TPU v7x, 256 devices: a whole 4x4x8 slice. The times are simulated.
256 devices in a mesh: seq: 64 (over y, z_hi, x, core), ch: 4 (over z_lo).
Axes of the slice: x: 4, y: 4, z: 8 (z_hi: 2, z_lo: 4; z = z_hi * 4 + z_lo), core: 2. Of those that a mesh axis runs over, the one named last changes fastest.
Arguments:
- token_ids: int32 [8192], P('seq'), may hold values from 0 to 511
- embedding: bfloat16 [512, 4096], P(None, 'ch'), may hold values from -6 to 6
- short_filter: float32 [7, 4096], P(None, 'ch'), may hold values from -2 to 2
- medium_filter: float32 [128, 4096], P(None, 'ch'), may hold values from -0.5 to 0.5
- long_residue: float32 [16, 4096], P(None, 'ch'), may hold values from -10.5 to 10.5, as said below
- long_rate: float32 [16, 4096], P(None, 'ch'), may hold values from 1e-05 to 0.05
- query_gain: float32 [4096], P('ch'), may hold values from -14 to 14
- key_gain: float32 [4096], P('ch'), may hold values from -14 to 14
Outputs:
- hyena_out: bfloat16 [8192, 4096], P('seq', 'ch')
- attended: bfloat16 [8192, 4096], P('seq', 'ch')
Inputs may be any that keep to these rules, and one draw needn't show every extreme that they name: `long_residue`: residues of the long filter's modes.
All inputs are finite; a program needn't handle non-finite values.
Results may differ from a plain program's by a relative error of at most 0.0095.
The roundings to bfloat16 on the way count: a program that leaves them out, or rounds other values in their place, can miss the bound.
Values may be sent and summed in bfloat16 or wider, within the bound.
A program may use at most 64 MiB of HBM per device.

v0:
```python
import math

import jax
import jax.numpy as jnp
from jax import lax
from jax.sharding import PartitionSpec as P

C = 4096
HEAD = 128


def shifted(value, axis, steps):
    count = lax.axis_size(axis)
    leading, last = (max(0, -steps), min(count, count - steps))
    return lax.ppermute(value, axis, [(source, source + steps) for source in range(leading, last)])


def swapped(shard, axis, apart):
    return lax.ppermute(shard, axis, [(i, i ^ 1 << apart) for i in range(lax.axis_size(axis))])


def from_behind(shard, axis, by):
    size = lax.axis_size(axis)
    return lax.ppermute(shard, axis, [(i, (i + by) % size) for i in range(size)])


def rounded(value):
    return lax.optimization_barrier(value.astype(jnp.bfloat16))


def depthwise_conv(widened, tap_weights, row_count):
    tap_count = tap_weights.shape[0]

    def add_tap(tap_index, running):
        window = lax.dynamic_slice_in_dim(widened, tap_count - 1 - tap_index, row_count, 0)
        return running + tap_weights[tap_index] * window.astype(jnp.float32)

    return lax.fori_loop(
        0, tap_count, add_tap, jnp.zeros((row_count, widened.shape[1]), jnp.float32)
    )


def long_kernel_rows(residue_mine, rate_mine, length):
    positions = jnp.arange(length, dtype=jnp.int32).astype(jnp.float32)
    mode_total = rate_mine.shape[0]

    def add_mode(mode_index, running):
        decay_rate = rate_mine[mode_index]
        mode_weight = (
            residue_mine[mode_index]
            * jnp.sqrt(-jnp.expm1(-2.0 * decay_rate))
            / math.sqrt(mode_total)
        )
        return running + mode_weight[:, None] * jnp.exp(-decay_rate[:, None] * positions[None, :])

    return lax.fori_loop(
        0, mode_total, add_mode, jnp.zeros((rate_mine.shape[1], length), jnp.float32)
    )


def dft_tables(row_size, column_size, period_size):
    row_index = lax.broadcasted_iota(jnp.int32, (row_size, column_size), 0)
    column_index = lax.broadcasted_iota(jnp.int32, (row_size, column_size), 1)
    angles = (row_index * column_index % period_size).astype(jnp.float32) * (
        2.0 * math.pi / period_size
    )
    return (jnp.cos(angles), jnp.sin(angles))


def forward_dft(signal, outer_size, inner_size):
    highest = lax.Precision.HIGHEST
    cos_outer, sin_outer = dft_tables(outer_size // 2, outer_size, outer_size)
    twiddle_cos, twiddle_sin = dft_tables(outer_size, inner_size, outer_size * inner_size)
    cos_inner, sin_inner = dft_tables(inner_size, inner_size, inner_size)
    step_real = jnp.einsum("pab,ak->pkb", signal, cos_outer, precision=highest)
    step_imag = -jnp.einsum("pab,ak->pkb", signal, sin_outer, precision=highest)
    turned_real = step_real * twiddle_cos + step_imag * twiddle_sin
    turned_imag = step_imag * twiddle_cos - step_real * twiddle_sin
    spec_real = jnp.einsum("pkb,bm->pkm", turned_real, cos_inner, precision=highest) + jnp.einsum(
        "pkb,bm->pkm", turned_imag, sin_inner, precision=highest
    )
    spec_imag = jnp.einsum("pkb,bm->pkm", turned_imag, cos_inner, precision=highest) - jnp.einsum(
        "pkb,bm->pkm", turned_real, sin_inner, precision=highest
    )
    return (spec_real, spec_imag)


def inverse_dft(spec_real, spec_imag, outer_size, inner_size):
    highest = lax.Precision.HIGHEST
    cos_outer, sin_outer = dft_tables(outer_size // 2, outer_size, outer_size)
    twiddle_cos, twiddle_sin = dft_tables(outer_size, inner_size, outer_size * inner_size)
    cos_inner, sin_inner = dft_tables(inner_size, inner_size, inner_size)
    back_real = jnp.einsum("pkm,mb->pkb", spec_real, cos_inner, precision=highest) - jnp.einsum(
        "pkm,mb->pkb", spec_imag, sin_inner, precision=highest
    )
    back_imag = jnp.einsum("pkm,mb->pkb", spec_real, sin_inner, precision=highest) + jnp.einsum(
        "pkm,mb->pkb", spec_imag, cos_inner, precision=highest
    )
    turned_real = back_real * twiddle_cos - back_imag * twiddle_sin
    turned_imag = back_real * twiddle_sin + back_imag * twiddle_cos
    signal = jnp.einsum("pkb,ak->pab", turned_real, cos_outer, precision=highest) - jnp.einsum(
        "pkb,ak->pab", turned_imag, sin_outer, precision=highest
    )
    return signal / (outer_size * inner_size)


def attend_block(query_rows, query_index, key_block, value_block, key_start, running, score_scale):
    row_peak, row_total, blended = running
    scores = (
        jnp.einsum("qhd,khd->hqk", query_rows, key_block, preferred_element_type=jnp.float32)
        * score_scale
    )
    key_index = key_start + jnp.arange(key_block.shape[0], dtype=jnp.int32)
    scores = jnp.where(key_index[None, None, :] <= query_index[None, :, None], scores, -1e30)
    new_peak = jnp.maximum(row_peak, jnp.max(scores, axis=2))
    weights = jnp.exp(scores - new_peak[:, :, None])
    rescale = jnp.exp(row_peak - new_peak)
    row_total = row_total * rescale + jnp.sum(weights, axis=2)
    blended = blended * rescale[:, :, None] + jnp.einsum(
        "hqk,khd->hqd",
        weights.astype(jnp.bfloat16),
        value_block,
        preferred_element_type=jnp.float32,
    )
    return (new_peak, row_total, blended)


def merge_partials(first_part, second_part):
    peak_one, total_one, blend_one = first_part
    peak_two, total_two, blend_two = second_part
    new_peak = jnp.maximum(peak_one, peak_two)
    scale_one = jnp.exp(peak_one - new_peak)
    scale_two = jnp.exp(peak_two - new_peak)
    new_total = total_one * scale_one + total_two * scale_two
    new_blend = blend_one * scale_one[..., None] + blend_two * scale_two[..., None]
    return (new_peak, new_total, new_blend)


def split_halves(stacked_part, half_size, upper_side):
    lower_half = stacked_part[:, :half_size]
    upper_half = stacked_part[:, half_size:]
    keep_half = jnp.where(upper_side == 1, upper_half, lower_half)
    send_half = jnp.where(upper_side == 1, lower_half, upper_half)
    return (keep_half, send_half)


def on_device(
    token_ids, embedding, short_filter, medium_filter, long_residue, long_rate, query_gain, key_gain
):
    tok_count = token_ids.shape[0]
    vocab_size = embedding.shape[0]
    width_dev = embedding.shape[1]
    seq_count = lax.axis_size("seq")
    seq_index = lax.axis_index("seq")
    one_hot = (
        token_ids[:, None] == lax.broadcasted_iota(jnp.int32, (tok_count, vocab_size), 1)
    ).astype(jnp.bfloat16)
    embedded = jnp.dot(one_hot, embedding, preferred_element_type=jnp.float32).astype(jnp.bfloat16)
    short_taps = short_filter.shape[0]
    rim_rows = shifted(embedded[tok_count - (short_taps - 1) :], "seq", 1)
    widened = jnp.concatenate([rim_rows, embedded], axis=0)
    short_part = depthwise_conv(widened, short_filter, tok_count)
    short_gated = rounded(embedded.astype(jnp.float32) * short_part)
    medium_taps = medium_filter.shape[0]
    upper_rows = shifted(short_gated[tok_count - (medium_taps - 1) :], "seq", 1)
    widened_two = jnp.concatenate([upper_rows, short_gated], axis=0)
    medium_part = depthwise_conv(widened_two, medium_filter, tok_count)
    medium_gated = rounded(short_gated.astype(jnp.float32) * medium_part)
    per_dev = width_dev // seq_count
    length = tok_count * seq_count
    grouped = medium_gated.T.reshape(seq_count, per_dev, tok_count)
    spread = lax.all_to_all(grouped, "seq", split_axis=0, concat_axis=2, tiled=True).reshape(
        per_dev, length
    )
    rate_mine = lax.dynamic_slice_in_dim(long_rate, seq_index * per_dev, per_dev, 1)
    residue_mine = lax.dynamic_slice_in_dim(long_residue, seq_index * per_dev, per_dev, 1)
    kernel = long_kernel_rows(residue_mine, rate_mine, length)
    outer_size = 128
    inner_size = 2 * length // outer_size
    spread_float = spread.astype(jnp.float32)
    data_real, data_imag = forward_dft(
        spread_float.reshape(per_dev, outer_size // 2, inner_size), outer_size, inner_size
    )
    kernel_real, kernel_imag = forward_dft(
        kernel.reshape(per_dev, outer_size // 2, inner_size), outer_size, inner_size
    )
    product_real = data_real * kernel_real - data_imag * kernel_imag
    product_imag = data_real * kernel_imag + data_imag * kernel_real
    long_part = inverse_dft(product_real, product_imag, outer_size, inner_size).reshape(
        per_dev, length
    )
    channel_out = (spread_float * long_part).astype(jnp.bfloat16)
    returned = lax.all_to_all(channel_out[None], "seq", split_axis=2, concat_axis=0, tiled=True)
    hyena_out = returned.reshape(width_dev, tok_count).T
    head_count = width_dev // HEAD
    hyena_float = hyena_out.astype(jnp.float32)
    square_sums = jnp.sum(hyena_float * hyena_float, axis=1)
    total_sums = lax.psum(square_sums, "ch")
    inverse_scale = lax.rsqrt(total_sums / C + 1e-05)
    normed = hyena_float * inverse_scale[:, None]
    values = normed.astype(jnp.bfloat16).reshape(tok_count, head_count, HEAD)
    queries = (
        (normed * query_gain[None, :]).astype(jnp.bfloat16).reshape(tok_count, head_count, HEAD)
    )
    key_rows = (
        (normed * key_gain[None, :]).astype(jnp.bfloat16).reshape(tok_count, head_count, HEAD)
    )
    group_size = 2
    level_count = group_size.bit_length() - 1
    seq_bits = seq_count.bit_length() - 1
    base_bit = seq_bits - level_count
    stride = seq_count // group_size
    stacked = queries[None]
    level = 0
    bit_number = base_bit + level
    partner_rows = swapped(stacked, "seq", bit_number)
    upper_side = seq_index >> bit_number & 1
    stacked = jnp.where(
        upper_side == 1,
        jnp.concatenate([partner_rows, stacked], axis=0),
        jnp.concatenate([stacked, partner_rows], axis=0),
    )
    query_rows = stacked.reshape(group_size * tok_count, head_count, HEAD)
    group_first = seq_index % stride
    block_numbers = group_first + stride * jnp.arange(group_size, dtype=jnp.int32)
    query_index = (
        block_numbers[:, None] * tok_count + jnp.arange(tok_count, dtype=jnp.int32)[None, :]
    ).reshape(group_size * tok_count)
    score_scale = HEAD ** (-0.5)
    partial_state = (
        jnp.full((head_count, group_size * tok_count), -1e30, jnp.float32),
        jnp.zeros((head_count, group_size * tok_count), jnp.float32),
        jnp.zeros((head_count, group_size * tok_count, HEAD), jnp.float32),
    )

    def cycle_step(turn_number, carried):
        key_block, value_block, running = carried
        key_block, value_block = from_behind((key_block, value_block), "seq", -1)
        source_block = jnp.remainder(seq_index + turn_number, seq_count)
        running = attend_block(
            query_rows,
            query_index,
            key_block,
            value_block,
            source_block * tok_count,
            running,
            score_scale,
        )
        return (key_block, value_block, running)

    carried = lax.fori_loop(1, stride + 1, cycle_step, (key_rows, values, partial_state))
    row_peak, row_total, blended = carried[2]
    row_peak = row_peak.reshape(head_count, group_size, tok_count)
    row_total = row_total.reshape(head_count, group_size, tok_count)
    blended = blended.reshape(head_count, group_size, tok_count, HEAD)
    for level in reversed(range(level_count)):
        bit_number = base_bit + level
        half_size = row_peak.shape[1] // 2
        upper_side = seq_index >> bit_number & 1
        keep_peak, send_peak = split_halves(row_peak, half_size, upper_side)
        keep_total, send_total = split_halves(row_total, half_size, upper_side)
        keep_blend, send_blend = split_halves(blended, half_size, upper_side)
        got_peak, got_total, got_blend = swapped(
            (send_peak, send_total, send_blend), "seq", bit_number
        )
        row_peak, row_total, blended = merge_partials(
            (keep_peak, keep_total, keep_blend), (got_peak, got_total, got_blend)
        )
    normalized = blended[:, 0] / row_total[:, 0][:, :, None]
    attended = normalized.transpose(1, 0, 2).reshape(tok_count, width_dev).astype(jnp.bfloat16)
    return (hyena_out, attended)


def solution(mesh):
    in_specs = (
        P("seq"),
        P(None, "ch"),
        P(None, "ch"),
        P(None, "ch"),
        P(None, "ch"),
        P(None, "ch"),
        P("ch"),
        P("ch"),
    )
    out_specs = (P("seq", "ch"), P("seq", "ch"))
    return jax.shard_map(
        on_device, mesh=mesh, in_specs=in_specs, out_specs=out_specs, check_vma=False
    )
```

profile of v0, /device:TPU:175, one launch (start us, length us, event | category | flops | bytes accessed | tf_op | source)
XLA Modules:
  0.0 1249.5 jit_solution(12640897642096204105)
XLA Ops:
  17.1 23.0 %while.70 = (s32[]{:T(128)}, f32[128,1024]{1,0:T(8,128)}, f32[7,1024]{1,0:T(8,128)}, bf16[134,1024]{1,0:T(8,128)(2,1)S(1)}, s32[]{:T(128)}, /*index=5*/s32[]{:T(128)}, s32[]{:T(128)}, s32[]{:T(128)}) while((s32[]{:T(128)}, f32[128,1024]{1,0:T(8,128)}, f32[7,1024]{1,0:T(8,128)}, bf16[134,1024]{1,0:T(8,128)(2,1)S(1)}, s32[]{:T(128)}, ...), condition=%wide.region_1.0_spmd.clone, body=%wide.region_0.0_spmd.clone.sunk | while | flops 524295 | bytes 1323157 | solution.py:38
  47.6 360.3 %while.71 = (s32[]{:T(128)}, f32[128,1024]{1,0:T(8,128)}, f32[128,1024]{1,0:T(8,128)}, bf16[255,1024]{1,0:T(8,128)(2,1)}, s32[]{:T(128)}, /*index=5*/s32[]{:T(128)}, s32[]{:T(128)}, s32[]{:T(128)}) while((s32[]{:T(128)}, f32[128,1024]{1,0:T(8,128)}, f32[128,1024]{1,0:T(8,128)}, bf16[255,1024]{1,0:T(8,128)(2,1)}, s32[]{:T(128)}, ...), condition=%wide.region_3.0_spmd.clone, body=%wide.region_2.0_spmd.clone.sunk | while | flops 524295 | bytes 1323157 | solution.py:38
  411.5 21.1 %all-to-all-start = ((bf16[64,16,128]{2,1,0:T(8,128)(2,1)}), bf16[64,16,128]{2,1,0:T(8,128)(2,1)S(1)}, u32[]{:S(2)}, u32[]{:S(2)}) async-start(bf16[64,16,128]{2,1,0:T(8,128)(2,1)} %bitcast.165), calls=%async_computation | async-start | bytes 524288 | tf_op jit(solution)/shard_map/all_to_all | solution.py:172
  462.9 45.2 %reduce = bf16[8192,16]{1,0:T(8,128)(2,1)S(1)} reduce(bf16[8192,1,16]{2,1,0:T(2,128)(2,1)} %bitcast.156, bf16[]{:T(256)} %broadcast.393), dimensions={1}, to_apply=%bitcast.121.reduce_sub_computation | reduce | bytes 524290
  510.4 19.1 %all_to_all.30 = bf16[64,2,1024]{2,1,0:T(2,128)(2,1)S(1)} all-to-all(bf16[64,2,1024]{2,1,0:T(2,128)(2,1)S(1)} %reshape.215), channel_id=1, replica_groups=mesh['seq'=64,'ch'=4] {'seq'}, dimensions={0} | all-to-all | bytes 524288 | tf_op jit(solution)/shard_map/all_to_all | solution.py:193
  560.7 611.1 %while.73 = (s32[]{:T(128)}, bf16[128,8,128]{2,0,1:T(8,128)(2,1)}, bf16[128,8,128]{2,0,1:T(8,128)(2,1)}, f32[8,256]{1,0:T(8,128)S(1)}, f32[8,256]{1,0:T(8,128)S(...) while((s32[]{:T(128)}, bf16[128,8,128]{2,0,1:T(8,128)(2,1)}, ...), condition=%wide.region_11.12_spmd.clone, body=%wide.region_8.11_spmd.clone.sunk | while | flops 136882576 | bytes 9637242 | solution.py:251
  565.0 15.1 %collective-permute-done = bf16[128,8,128]{2,0,1:T(8,128)(2,1)S(1)} collective-permute-done((bf16[128,8,128]{2,0,1:T(8,128)(2,1)}, bf16[128,8,128]{2,0,1:T(8,128)(2,1)S(1)}, u32[]{:S(2)}, u32[]{:S(2)}) %collective-permute-start) | collective-permute-done | bytes 262176 | tf_op jit(solution)/shard_map/while/body/eval_jaxpr/ppermute | solution.py:24
  584.7 13.6 %collective-permute-done = bf16[128,8,128]{2,0,1:T(8,128)(2,1)S(1)} collective-permute-done((bf16[128,8,128]{2,0,1:T(8,128)(2,1)}, bf16[128,8,128]{2,0,1:T(8,128)(2,1)S(1)}, u32[]{:S(2)}, u32[]{:S(2)}) %collective-permute-start) | collective-permute-done | bytes 262176 | tf_op jit(solution)/shard_map/while/body/eval_jaxpr/ppermute | solution.py:24
  602.9 12.7 %collective-permute-done = bf16[128,8,128]{2,0,1:T(8,128)(2,1)S(1)} collective-permute-done((bf16[128,8,128]{2,0,1:T(8,128)(2,1)}, bf16[128,8,128]{2,0,1:T(8,128)(2,1)S(1)}, u32[]{:S(2)}, u32[]{:S(2)}) %collective-permute-start) | collective-permute-done | bytes 262176 | tf_op jit(solution)/shard_map/while/body/eval_jaxpr/ppermute | solution.py:24
  620.2 12.6 %collective-permute-done = bf16[128,8,128]{2,0,1:T(8,128)(2,1)S(1)} collective-permute-done((bf16[128,8,128]{2,0,1:T(8,128)(2,1)}, bf16[128,8,128]{2,0,1:T(8,128)(2,1)S(1)}, u32[]{:S(2)}, u32[]{:S(2)}) %collective-permute-start) | collective-permute-done | bytes 262176 | tf_op jit(solution)/shard_map/while/body/eval_jaxpr/ppermute | solution.py:24
  637.4 12.6 %collective-permute-done = bf16[128,8,128]{2,0,1:T(8,128)(2,1)S(1)} collective-permute-done((bf16[128,8,128]{2,0,1:T(8,128)(2,1)}, bf16[128,8,128]{2,0,1:T(8,128)(2,1)S(1)}, u32[]{:S(2)}, u32[]{:S(2)}) %collective-permute-start) | collective-permute-done | bytes 262176 | tf_op jit(solution)/shard_map/while/body/eval_jaxpr/ppermute | solution.py:24
  654.7 12.6 %collective-permute-done = bf16[128,8,128]{2,0,1:T(8,128)(2,1)S(1)} collective-permute-done((bf16[128,8,128]{2,0,1:T(8,128)(2,1)}, bf16[128,8,128]{2,0,1:T(8,128)(2,1)S(1)}, u32[]{:S(2)}, u32[]{:S(2)}) %collective-permute-start) | collective-permute-done | bytes 262176 | tf_op jit(solution)/shard_map/while/body/eval_jaxpr/ppermute | solution.py:24
  672.4 12.7 %collective-permute-done = bf16[128,8,128]{2,0,1:T(8,128)(2,1)S(1)} collective-permute-done((bf16[128,8,128]{2,0,1:T(8,128)(2,1)}, bf16[128,8,128]{2,0,1:T(8,128)(2,1)S(1)}, u32[]{:S(2)}, u32[]{:S(2)}) %collective-permute-start) | collective-permute-done | bytes 262176 | tf_op jit(solution)/shard_map/while/body/eval_jaxpr/ppermute | solution.py:24
  695.3 16.8 %collective-permute-done = bf16[128,8,128]{2,0,1:T(8,128)(2,1)S(1)} collective-permute-done((bf16[128,8,128]{2,0,1:T(8,128)(2,1)}, bf16[128,8,128]{2,0,1:T(8,128)(2,1)S(1)}, u32[]{:S(2)}, u32[]{:S(2)}) %collective-permute-start) | collective-permute-done | bytes 262176 | tf_op jit(solution)/shard_map/while/body/eval_jaxpr/ppermute | solution.py:24
  716.7 12.7 %collective-permute-done = bf16[128,8,128]{2,0,1:T(8,128)(2,1)S(1)} collective-permute-done((bf16[128,8,128]{2,0,1:T(8,128)(2,1)}, bf16[128,8,128]{2,0,1:T(8,128)(2,1)S(1)}, u32[]{:S(2)}, u32[]{:S(2)}) %collective-permute-start) | collective-permute-done | bytes 262176 | tf_op jit(solution)/shard_map/while/body/eval_jaxpr/ppermute | solution.py:24
  768.6 12.6 %collective-permute-done = bf16[128,8,128]{2,0,1:T(8,128)(2,1)S(1)} collective-permute-done((bf16[128,8,128]{2,0,1:T(8,128)(2,1)}, bf16[128,8,128]{2,0,1:T(8,128)(2,1)S(1)}, u32[]{:S(2)}, u32[]{:S(2)}) %collective-permute-start) | collective-permute-done | bytes 262176 | tf_op jit(solution)/shard_map/while/body/eval_jaxpr/ppermute | solution.py:24
  803.3 12.6 %collective-permute-done = bf16[128,8,128]{2,0,1:T(8,128)(2,1)S(1)} collective-permute-done((bf16[128,8,128]{2,0,1:T(8,128)(2,1)}, bf16[128,8,128]{2,0,1:T(8,128)(2,1)S(1)}, u32[]{:S(2)}, u32[]{:S(2)}) %collective-permute-start) | collective-permute-done | bytes 262176 | tf_op jit(solution)/shard_map/while/body/eval_jaxpr/ppermute | solution.py:24
  820.8 12.7 %collective-permute-done = bf16[128,8,128]{2,0,1:T(8,128)(2,1)S(1)} collective-permute-done((bf16[128,8,128]{2,0,1:T(8,128)(2,1)}, bf16[128,8,128]{2,0,1:T(8,128)(2,1)S(1)}, u32[]{:S(2)}, u32[]{:S(2)}) %collective-permute-start) | collective-permute-done | bytes 262176 | tf_op jit(solution)/shard_map/while/body/eval_jaxpr/ppermute | solution.py:24
  843.7 17.0 %collective-permute-done = bf16[128,8,128]{2,0,1:T(8,128)(2,1)S(1)} collective-permute-done((bf16[128,8,128]{2,0,1:T(8,128)(2,1)}, bf16[128,8,128]{2,0,1:T(8,128)(2,1)S(1)}, u32[]{:S(2)}, u32[]{:S(2)}) %collective-permute-start) | collective-permute-done | bytes 262176 | tf_op jit(solution)/shard_map/while/body/eval_jaxpr/ppermute | solution.py:24
  865.2 12.7 %collective-permute-done = bf16[128,8,128]{2,0,1:T(8,128)(2,1)S(1)} collective-permute-done((bf16[128,8,128]{2,0,1:T(8,128)(2,1)}, bf16[128,8,128]{2,0,1:T(8,128)(2,1)S(1)}, u32[]{:S(2)}, u32[]{:S(2)}) %collective-permute-start) | collective-permute-done | bytes 262176 | tf_op jit(solution)/shard_map/while/body/eval_jaxpr/ppermute | solution.py:24
  882.6 12.6 %collective-permute-done = bf16[128,8,128]{2,0,1:T(8,128)(2,1)S(1)} collective-permute-done((bf16[128,8,128]{2,0,1:T(8,128)(2,1)}, bf16[128,8,128]{2,0,1:T(8,128)(2,1)S(1)}, u32[]{:S(2)}, u32[]{:S(2)}) %collective-permute-start) | collective-permute-done | bytes 262176 | tf_op jit(solution)/shard_map/while/body/eval_jaxpr/ppermute | solution.py:24
  934.5 12.6 %collective-permute-done = bf16[128,8,128]{2,0,1:T(8,128)(2,1)S(1)} collective-permute-done((bf16[128,8,128]{2,0,1:T(8,128)(2,1)}, bf16[128,8,128]{2,0,1:T(8,128)(2,1)S(1)}, u32[]{:S(2)}, u32[]{:S(2)}) %collective-permute-start) | collective-permute-done | bytes 262176 | tf_op jit(solution)/shard_map/while/body/eval_jaxpr/ppermute | solution.py:24
  969.2 12.7 %collective-permute-done = bf16[128,8,128]{2,0,1:T(8,128)(2,1)S(1)} collective-permute-done((bf16[128,8,128]{2,0,1:T(8,128)(2,1)}, bf16[128,8,128]{2,0,1:T(8,128)(2,1)S(1)}, u32[]{:S(2)}, u32[]{:S(2)}) %collective-permute-start) | collective-permute-done | bytes 262176 | tf_op jit(solution)/shard_map/while/body/eval_jaxpr/ppermute | solution.py:24
  992.1 17.1 %collective-permute-done = bf16[128,8,128]{2,0,1:T(8,128)(2,1)S(1)} collective-permute-done((bf16[128,8,128]{2,0,1:T(8,128)(2,1)}, bf16[128,8,128]{2,0,1:T(8,128)(2,1)S(1)}, u32[]{:S(2)}, u32[]{:S(2)}) %collective-permute-start) | collective-permute-done | bytes 262176 | tf_op jit(solution)/shard_map/while/body/eval_jaxpr/ppermute | solution.py:24
  1013.8 15.5 %collective-permute-done = bf16[128,8,128]{2,0,1:T(8,128)(2,1)S(1)} collective-permute-done((bf16[128,8,128]{2,0,1:T(8,128)(2,1)}, bf16[128,8,128]{2,0,1:T(8,128)(2,1)S(1)}, u32[]{:S(2)}, u32[]{:S(2)}) %collective-permute-start) | collective-permute-done | bytes 262176 | tf_op jit(solution)/shard_map/while/body/eval_jaxpr/ppermute | solution.py:24
  1033.9 14.6 %collective-permute-done = bf16[128,8,128]{2,0,1:T(8,128)(2,1)S(1)} collective-permute-done((bf16[128,8,128]{2,0,1:T(8,128)(2,1)}, bf16[128,8,128]{2,0,1:T(8,128)(2,1)S(1)}, u32[]{:S(2)}, u32[]{:S(2)}) %collective-permute-start) | collective-permute-done | bytes 262176 | tf_op jit(solution)/shard_map/while/body/eval_jaxpr/ppermute | solution.py:24
  1053.1 16.3 %collective-permute-done = bf16[128,8,128]{2,0,1:T(8,128)(2,1)S(1)} collective-permute-done((bf16[128,8,128]{2,0,1:T(8,128)(2,1)}, bf16[128,8,128]{2,0,1:T(8,128)(2,1)S(1)}, u32[]{:S(2)}, u32[]{:S(2)}) %collective-permute-start) | collective-permute-done | bytes 262176 | tf_op jit(solution)/shard_map/while/body/eval_jaxpr/ppermute | solution.py:24
  1074.0 18.2 %collective-permute-done = bf16[128,8,128]{2,0,1:T(8,128)(2,1)S(1)} collective-permute-done((bf16[128,8,128]{2,0,1:T(8,128)(2,1)}, bf16[128,8,128]{2,0,1:T(8,128)(2,1)S(1)}, u32[]{:S(2)}, u32[]{:S(2)}) %collective-permute-start) | collective-permute-done | bytes 262176 | tf_op jit(solution)/shard_map/while/body/eval_jaxpr/ppermute | solution.py:24
  1096.9 16.0 %collective-permute-done = bf16[128,8,128]{2,0,1:T(8,128)(2,1)S(1)} collective-permute-done((bf16[128,8,128]{2,0,1:T(8,128)(2,1)}, bf16[128,8,128]{2,0,1:T(8,128)(2,1)S(1)}, u32[]{:S(2)}, u32[]{:S(2)}) %collective-permute-start) | collective-permute-done | bytes 262176 | tf_op jit(solution)/shard_map/while/body/eval_jaxpr/ppermute | solution.py:24
  1117.5 15.0 %collective-permute-done = bf16[128,8,128]{2,0,1:T(8,128)(2,1)S(1)} collective-permute-done((bf16[128,8,128]{2,0,1:T(8,128)(2,1)}, bf16[128,8,128]{2,0,1:T(8,128)(2,1)S(1)}, u32[]{:S(2)}, u32[]{:S(2)}) %collective-permute-start) | collective-permute-done | bytes 262176 | tf_op jit(solution)/shard_map/while/body/eval_jaxpr/ppermute | solution.py:24
  1137.1 13.1 %collective-permute-done = bf16[128,8,128]{2,0,1:T(8,128)(2,1)S(1)} collective-permute-done((bf16[128,8,128]{2,0,1:T(8,128)(2,1)}, bf16[128,8,128]{2,0,1:T(8,128)(2,1)S(1)}, u32[]{:S(2)}, u32[]{:S(2)}) %collective-permute-start) | collective-permute-done | bytes 262176 | tf_op jit(solution)/shard_map/while/body/eval_jaxpr/ppermute | solution.py:24
  1171.8 65.1 %collective-permute-start.5 = (f32[8,1,128]{2,0,1:T(8,128)S(1)}, f32[8,1,128]{2,0,1:T(8,128)S(1)}, u32[]{:S(2)}, u32[]{:S(2)}) collective-permute-start(f32[8,1,128]{2,0,1:T(8,128)S(1)} %slice_select_fusion.1), channel_id=1, source_target_pairs={{0,128},{4,132},{8,136},{12,140},{16,144},{20,148},{24,152},{28,15... | collective-permute-start | bytes 12296 | tf_op jit(solution)/shard_map/ppermute | solution.py:19
  (866 shorter events, 745.1 us)
Async XLA Ops:
  411.5 29.9 %all-to-all-start = ((bf16[64,16,128]{2,1,0:T(8,128)(2,1)}), bf16[64,16,128]{2,1,0:T(8,128)(2,1)S(1)}, u32[]{:S(2)}, u32[]{:S(2)}) async-start(bf16[64,16,128]{2,1,0:T(8,128)(2,1)} %bitcast.165), calls=%async_computation | async-start | bytes 524288 | tf_op jit(solution)/shard_map/all_to_all | solution.py:172
  560.7 19.4 %collective-permute-start = (bf16[128,8,128]{2,0,1:T(8,128)(2,1)}, bf16[128,8,128]{2,0,1:T(8,128)(2,1)S(1)}, u32[]{:S(2)}, u32[]{:S(2)}) collective-permute-start(bf16[128,8,128]{2,0,1:T(8,128)(2,1)} %get-tuple-element.964), channel_id=1, source_target_pairs={{0,252},{4,0},{8,4},{12,8},{16,12},{20,16},{24,20},{28,24},{32,28}... | collective-permute-start | bytes 786440 | tf_op jit(solution)/shard_map/while/body/eval_jaxpr/ppermute | solution.py:24
  564.7 18.2 %collective-permute-start.1 = (bf16[128,8,128]{2,0,1:T(8,128)(2,1)}, bf16[128,8,128]{2,0,1:T(8,128)(2,1)S(1)}, u32[]{:S(2)}, u32[]{:S(2)}) collective-permute-start(bf16[128,8,128]{2,0,1:T(8,128)(2,1)} %get-tuple-element.965), channel_id=1, source_target_pairs={{0,252},{4,0},{8,4},{12,8},{16,12},{20,16},{24,20},{28,24},{32,28}... | collective-permute-start | bytes 786440 | tf_op jit(solution)/shard_map/while/body/eval_jaxpr/ppermute | solution.py:24
  584.4 16.7 %collective-permute-start.1 = (bf16[128,8,128]{2,0,1:T(8,128)(2,1)}, bf16[128,8,128]{2,0,1:T(8,128)(2,1)S(1)}, u32[]{:S(2)}, u32[]{:S(2)}) collective-permute-start(bf16[128,8,128]{2,0,1:T(8,128)(2,1)} %get-tuple-element.965), channel_id=1, source_target_pairs={{0,252},{4,0},{8,4},{12,8},{16,12},{20,16},{24,20},{28,24},{32,28}... | collective-permute-start | bytes 786440 | tf_op jit(solution)/shard_map/while/body/eval_jaxpr/ppermute | solution.py:24
  602.6 15.8 %collective-permute-start.1 = (bf16[128,8,128]{2,0,1:T(8,128)(2,1)}, bf16[128,8,128]{2,0,1:T(8,128)(2,1)S(1)}, u32[]{:S(2)}, u32[]{:S(2)}) collective-permute-start(bf16[128,8,128]{2,0,1:T(8,128)(2,1)} %get-tuple-element.965), channel_id=1, source_target_pairs={{0,252},{4,0},{8,4},{12,8},{16,12},{20,16},{24,20},{28,24},{32,28}... | collective-permute-start | bytes 786440 | tf_op jit(solution)/shard_map/while/body/eval_jaxpr/ppermute | solution.py:24
  654.4 16.2 %collective-permute-start.1 = (bf16[128,8,128]{2,0,1:T(8,128)(2,1)}, bf16[128,8,128]{2,0,1:T(8,128)(2,1)S(1)}, u32[]{:S(2)}, u32[]{:S(2)}) collective-permute-start(bf16[128,8,128]{2,0,1:T(8,128)(2,1)} %get-tuple-element.965), channel_id=1, source_target_pairs={{0,252},{4,0},{8,4},{12,8},{16,12},{20,16},{24,20},{28,24},{32,28}... | collective-permute-start | bytes 786440 | tf_op jit(solution)/shard_map/while/body/eval_jaxpr/ppermute | solution.py:24
  672.1 21.4 %collective-permute-start.1 = (bf16[128,8,128]{2,0,1:T(8,128)(2,1)}, bf16[128,8,128]{2,0,1:T(8,128)(2,1)S(1)}, u32[]{:S(2)}, u32[]{:S(2)}) collective-permute-start(bf16[128,8,128]{2,0,1:T(8,128)(2,1)} %get-tuple-element.965), channel_id=1, source_target_pairs={{0,252},{4,0},{8,4},{12,8},{16,12},{20,16},{24,20},{28,24},{32,28}... | collective-permute-start | bytes 786440 | tf_op jit(solution)/shard_map/while/body/eval_jaxpr/ppermute | solution.py:24
  694.9 17.1 %collective-permute-start = (bf16[128,8,128]{2,0,1:T(8,128)(2,1)}, bf16[128,8,128]{2,0,1:T(8,128)(2,1)S(1)}, u32[]{:S(2)}, u32[]{:S(2)}) collective-permute-start(bf16[128,8,128]{2,0,1:T(8,128)(2,1)} %get-tuple-element.964), channel_id=1, source_target_pairs={{0,252},{4,0},{8,4},{12,8},{16,12},{20,16},{24,20},{28,24},{32,28}... | collective-permute-start | bytes 786440 | tf_op jit(solution)/shard_map/while/body/eval_jaxpr/ppermute | solution.py:24
  695.0 19.9 %collective-permute-start.1 = (bf16[128,8,128]{2,0,1:T(8,128)(2,1)}, bf16[128,8,128]{2,0,1:T(8,128)(2,1)S(1)}, u32[]{:S(2)}, u32[]{:S(2)}) collective-permute-start(bf16[128,8,128]{2,0,1:T(8,128)(2,1)} %get-tuple-element.965), channel_id=1, source_target_pairs={{0,252},{4,0},{8,4},{12,8},{16,12},{20,16},{24,20},{28,24},{32,28}... | collective-permute-start | bytes 786440 | tf_op jit(solution)/shard_map/while/body/eval_jaxpr/ppermute | solution.py:24
  716.4 15.8 %collective-permute-start.1 = (bf16[128,8,128]{2,0,1:T(8,128)(2,1)}, bf16[128,8,128]{2,0,1:T(8,128)(2,1)S(1)}, u32[]{:S(2)}, u32[]{:S(2)}) collective-permute-start(bf16[128,8,128]{2,0,1:T(8,128)(2,1)} %get-tuple-element.965), channel_id=1, source_target_pairs={{0,252},{4,0},{8,4},{12,8},{16,12},{20,16},{24,20},{28,24},{32,28}... | collective-permute-start | bytes 786440 | tf_op jit(solution)/shard_map/while/body/eval_jaxpr/ppermute | solution.py:24
  733.7 15.8 %collective-permute-start.1 = (bf16[128,8,128]{2,0,1:T(8,128)(2,1)}, bf16[128,8,128]{2,0,1:T(8,128)(2,1)S(1)}, u32[]{:S(2)}, u32[]{:S(2)}) collective-permute-start(bf16[128,8,128]{2,0,1:T(8,128)(2,1)} %get-tuple-element.965), channel_id=1, source_target_pairs={{0,252},{4,0},{8,4},{12,8},{16,12},{20,16},{24,20},{28,24},{32,28}... | collective-permute-start | bytes 786440 | tf_op jit(solution)/shard_map/while/body/eval_jaxpr/ppermute | solution.py:24
  751.0 15.8 %collective-permute-start.1 = (bf16[128,8,128]{2,0,1:T(8,128)(2,1)}, bf16[128,8,128]{2,0,1:T(8,128)(2,1)S(1)}, u32[]{:S(2)}, u32[]{:S(2)}) collective-permute-start(bf16[128,8,128]{2,0,1:T(8,128)(2,1)} %get-tuple-element.965), channel_id=1, source_target_pairs={{0,252},{4,0},{8,4},{12,8},{16,12},{20,16},{24,20},{28,24},{32,28}... | collective-permute-start | bytes 786440 | tf_op jit(solution)/shard_map/while/body/eval_jaxpr/ppermute | solution.py:24
  803.0 16.0 %collective-permute-start.1 = (bf16[128,8,128]{2,0,1:T(8,128)(2,1)}, bf16[128,8,128]{2,0,1:T(8,128)(2,1)S(1)}, u32[]{:S(2)}, u32[]{:S(2)}) collective-permute-start(bf16[128,8,128]{2,0,1:T(8,128)(2,1)} %get-tuple-element.965), channel_id=1, source_target_pairs={{0,252},{4,0},{8,4},{12,8},{16,12},{20,16},{24,20},{28,24},{32,28}... | collective-permute-start | bytes 786440 | tf_op jit(solution)/shard_map/while/body/eval_jaxpr/ppermute | solution.py:24
  820.5 21.4 %collective-permute-start.1 = (bf16[128,8,128]{2,0,1:T(8,128)(2,1)}, bf16[128,8,128]{2,0,1:T(8,128)(2,1)S(1)}, u32[]{:S(2)}, u32[]{:S(2)}) collective-permute-start(bf16[128,8,128]{2,0,1:T(8,128)(2,1)} %get-tuple-element.965), channel_id=1, source_target_pairs={{0,252},{4,0},{8,4},{12,8},{16,12},{20,16},{24,20},{28,24},{32,28}... | collective-permute-start | bytes 786440 | tf_op jit(solution)/shard_map/while/body/eval_jaxpr/ppermute | solution.py:24
  843.3 17.3 %collective-permute-start = (bf16[128,8,128]{2,0,1:T(8,128)(2,1)}, bf16[128,8,128]{2,0,1:T(8,128)(2,1)S(1)}, u32[]{:S(2)}, u32[]{:S(2)}) collective-permute-start(bf16[128,8,128]{2,0,1:T(8,128)(2,1)} %get-tuple-element.964), channel_id=1, source_target_pairs={{0,252},{4,0},{8,4},{12,8},{16,12},{20,16},{24,20},{28,24},{32,28}... | collective-permute-start | bytes 786440 | tf_op jit(solution)/shard_map/while/body/eval_jaxpr/ppermute | solution.py:24
  843.4 20.1 %collective-permute-start.1 = (bf16[128,8,128]{2,0,1:T(8,128)(2,1)}, bf16[128,8,128]{2,0,1:T(8,128)(2,1)S(1)}, u32[]{:S(2)}, u32[]{:S(2)}) collective-permute-start(bf16[128,8,128]{2,0,1:T(8,128)(2,1)} %get-tuple-element.965), channel_id=1, source_target_pairs={{0,252},{4,0},{8,4},{12,8},{16,12},{20,16},{24,20},{28,24},{32,28}... | collective-permute-start | bytes 786440 | tf_op jit(solution)/shard_map/while/body/eval_jaxpr/ppermute | solution.py:24
  864.9 15.8 %collective-permute-start.1 = (bf16[128,8,128]{2,0,1:T(8,128)(2,1)}, bf16[128,8,128]{2,0,1:T(8,128)(2,1)S(1)}, u32[]{:S(2)}, u32[]{:S(2)}) collective-permute-start(bf16[128,8,128]{2,0,1:T(8,128)(2,1)} %get-tuple-element.965), channel_id=1, source_target_pairs={{0,252},{4,0},{8,4},{12,8},{16,12},{20,16},{24,20},{28,24},{32,28}... | collective-permute-start | bytes 786440 | tf_op jit(solution)/shard_map/while/body/eval_jaxpr/ppermute | solution.py:24
  968.9 21.4 %collective-permute-start.1 = (bf16[128,8,128]{2,0,1:T(8,128)(2,1)}, bf16[128,8,128]{2,0,1:T(8,128)(2,1)S(1)}, u32[]{:S(2)}, u32[]{:S(2)}) collective-permute-start(bf16[128,8,128]{2,0,1:T(8,128)(2,1)} %get-tuple-element.965), channel_id=1, source_target_pairs={{0,252},{4,0},{8,4},{12,8},{16,12},{20,16},{24,20},{28,24},{32,28}... | collective-permute-start | bytes 786440 | tf_op jit(solution)/shard_map/while/body/eval_jaxpr/ppermute | solution.py:24
  991.7 17.5 %collective-permute-start = (bf16[128,8,128]{2,0,1:T(8,128)(2,1)}, bf16[128,8,128]{2,0,1:T(8,128)(2,1)S(1)}, u32[]{:S(2)}, u32[]{:S(2)}) collective-permute-start(bf16[128,8,128]{2,0,1:T(8,128)(2,1)} %get-tuple-element.964), channel_id=1, source_target_pairs={{0,252},{4,0},{8,4},{12,8},{16,12},{20,16},{24,20},{28,24},{32,28}... | collective-permute-start | bytes 786440 | tf_op jit(solution)/shard_map/while/body/eval_jaxpr/ppermute | solution.py:24
  991.8 20.2 %collective-permute-start.1 = (bf16[128,8,128]{2,0,1:T(8,128)(2,1)}, bf16[128,8,128]{2,0,1:T(8,128)(2,1)S(1)}, u32[]{:S(2)}, u32[]{:S(2)}) collective-permute-start(bf16[128,8,128]{2,0,1:T(8,128)(2,1)} %get-tuple-element.965), channel_id=1, source_target_pairs={{0,252},{4,0},{8,4},{12,8},{16,12},{20,16},{24,20},{28,24},{32,28}... | collective-permute-start | bytes 786440 | tf_op jit(solution)/shard_map/while/body/eval_jaxpr/ppermute | solution.py:24
  1013.4 15.9 %collective-permute-start = (bf16[128,8,128]{2,0,1:T(8,128)(2,1)}, bf16[128,8,128]{2,0,1:T(8,128)(2,1)S(1)}, u32[]{:S(2)}, u32[]{:S(2)}) collective-permute-start(bf16[128,8,128]{2,0,1:T(8,128)(2,1)} %get-tuple-element.964), channel_id=1, source_target_pairs={{0,252},{4,0},{8,4},{12,8},{16,12},{20,16},{24,20},{28,24},{32,28}... | collective-permute-start | bytes 786440 | tf_op jit(solution)/shard_map/while/body/eval_jaxpr/ppermute | solution.py:24
  1013.5 18.6 %collective-permute-start.1 = (bf16[128,8,128]{2,0,1:T(8,128)(2,1)}, bf16[128,8,128]{2,0,1:T(8,128)(2,1)S(1)}, u32[]{:S(2)}, u32[]{:S(2)}) collective-permute-start(bf16[128,8,128]{2,0,1:T(8,128)(2,1)} %get-tuple-element.965), channel_id=1, source_target_pairs={{0,252},{4,0},{8,4},{12,8},{16,12},{20,16},{24,20},{28,24},{32,28}... | collective-permute-start | bytes 786440 | tf_op jit(solution)/shard_map/while/body/eval_jaxpr/ppermute | solution.py:24
  1033.6 17.7 %collective-permute-start.1 = (bf16[128,8,128]{2,0,1:T(8,128)(2,1)}, bf16[128,8,128]{2,0,1:T(8,128)(2,1)S(1)}, u32[]{:S(2)}, u32[]{:S(2)}) collective-permute-start(bf16[128,8,128]{2,0,1:T(8,128)(2,1)} %get-tuple-element.965), channel_id=1, source_target_pairs={{0,252},{4,0},{8,4},{12,8},{16,12},{20,16},{24,20},{28,24},{32,28}... | collective-permute-start | bytes 786440 | tf_op jit(solution)/shard_map/while/body/eval_jaxpr/ppermute | solution.py:24
  1052.7 16.7 %collective-permute-start = (bf16[128,8,128]{2,0,1:T(8,128)(2,1)}, bf16[128,8,128]{2,0,1:T(8,128)(2,1)S(1)}, u32[]{:S(2)}, u32[]{:S(2)}) collective-permute-start(bf16[128,8,128]{2,0,1:T(8,128)(2,1)} %get-tuple-element.964), channel_id=1, source_target_pairs={{0,252},{4,0},{8,4},{12,8},{16,12},{20,16},{24,20},{28,24},{32,28}... | collective-permute-start | bytes 786440 | tf_op jit(solution)/shard_map/while/body/eval_jaxpr/ppermute | solution.py:24
  1052.8 19.4 %collective-permute-start.1 = (bf16[128,8,128]{2,0,1:T(8,128)(2,1)}, bf16[128,8,128]{2,0,1:T(8,128)(2,1)S(1)}, u32[]{:S(2)}, u32[]{:S(2)}) collective-permute-start(bf16[128,8,128]{2,0,1:T(8,128)(2,1)} %get-tuple-element.965), channel_id=1, source_target_pairs={{0,252},{4,0},{8,4},{12,8},{16,12},{20,16},{24,20},{28,24},{32,28}... | collective-permute-start | bytes 786440 | tf_op jit(solution)/shard_map/while/body/eval_jaxpr/ppermute | solution.py:24
  1073.6 18.6 %collective-permute-start = (bf16[128,8,128]{2,0,1:T(8,128)(2,1)}, bf16[128,8,128]{2,0,1:T(8,128)(2,1)S(1)}, u32[]{:S(2)}, u32[]{:S(2)}) collective-permute-start(bf16[128,8,128]{2,0,1:T(8,128)(2,1)} %get-tuple-element.964), channel_id=1, source_target_pairs={{0,252},{4,0},{8,4},{12,8},{16,12},{20,16},{24,20},{28,24},{32,28}... | collective-permute-start | bytes 786440 | tf_op jit(solution)/shard_map/while/body/eval_jaxpr/ppermute | solution.py:24
  1073.7 21.3 %collective-permute-start.1 = (bf16[128,8,128]{2,0,1:T(8,128)(2,1)}, bf16[128,8,128]{2,0,1:T(8,128)(2,1)S(1)}, u32[]{:S(2)}, u32[]{:S(2)}) collective-permute-start(bf16[128,8,128]{2,0,1:T(8,128)(2,1)} %get-tuple-element.965), channel_id=1, source_target_pairs={{0,252},{4,0},{8,4},{12,8},{16,12},{20,16},{24,20},{28,24},{32,28}... | collective-permute-start | bytes 786440 | tf_op jit(solution)/shard_map/while/body/eval_jaxpr/ppermute | solution.py:24
  1096.5 16.4 %collective-permute-start = (bf16[128,8,128]{2,0,1:T(8,128)(2,1)}, bf16[128,8,128]{2,0,1:T(8,128)(2,1)S(1)}, u32[]{:S(2)}, u32[]{:S(2)}) collective-permute-start(bf16[128,8,128]{2,0,1:T(8,128)(2,1)} %get-tuple-element.964), channel_id=1, source_target_pairs={{0,252},{4,0},{8,4},{12,8},{16,12},{20,16},{24,20},{28,24},{32,28}... | collective-permute-start | bytes 786440 | tf_op jit(solution)/shard_map/while/body/eval_jaxpr/ppermute | solution.py:24
  1096.6 19.1 %collective-permute-start.1 = (bf16[128,8,128]{2,0,1:T(8,128)(2,1)}, bf16[128,8,128]{2,0,1:T(8,128)(2,1)S(1)}, u32[]{:S(2)}, u32[]{:S(2)}) collective-permute-start(bf16[128,8,128]{2,0,1:T(8,128)(2,1)} %get-tuple-element.965), channel_id=1, source_target_pairs={{0,252},{4,0},{8,4},{12,8},{16,12},{20,16},{24,20},{28,24},{32,28}... | collective-permute-start | bytes 786440 | tf_op jit(solution)/shard_map/while/body/eval_jaxpr/ppermute | solution.py:24
  1117.2 18.1 %collective-permute-start.1 = (bf16[128,8,128]{2,0,1:T(8,128)(2,1)}, bf16[128,8,128]{2,0,1:T(8,128)(2,1)S(1)}, u32[]{:S(2)}, u32[]{:S(2)}) collective-permute-start(bf16[128,8,128]{2,0,1:T(8,128)(2,1)} %get-tuple-element.965), channel_id=1, source_target_pairs={{0,252},{4,0},{8,4},{12,8},{16,12},{20,16},{24,20},{28,24},{32,28}... | collective-permute-start | bytes 786440 | tf_op jit(solution)/shard_map/while/body/eval_jaxpr/ppermute | solution.py:24
  1136.8 16.3 %collective-permute-start.1 = (bf16[128,8,128]{2,0,1:T(8,128)(2,1)}, bf16[128,8,128]{2,0,1:T(8,128)(2,1)S(1)}, u32[]{:S(2)}, u32[]{:S(2)}) collective-permute-start(bf16[128,8,128]{2,0,1:T(8,128)(2,1)} %get-tuple-element.965), channel_id=1, source_target_pairs={{0,252},{4,0},{8,4},{12,8},{16,12},{20,16},{24,20},{28,24},{32,28}... | collective-permute-start | bytes 786440 | tf_op jit(solution)/shard_map/while/body/eval_jaxpr/ppermute | solution.py:24
  1171.8 68.9 %collective-permute-start.5 = (f32[8,1,128]{2,0,1:T(8,128)S(1)}, f32[8,1,128]{2,0,1:T(8,128)S(1)}, u32[]{:S(2)}, u32[]{:S(2)}) collective-permute-start(f32[8,1,128]{2,0,1:T(8,128)S(1)} %slice_select_fusion.1), channel_id=1, source_target_pairs={{0,128},{4,132},{8,136},{12,140},{16,144},{20,148},{24,152},{28,15... | collective-permute-start | bytes 12296 | tf_op jit(solution)/shard_map/ppermute | solution.py:19
  (45 other events, 560.1 us)
where the time goes:
time: 1270 us; the launch traced here: 1250 us
  waiting for transfers between devices  526 us (41%)
  other arithmetic  344 us (27%)
  local copies, waits for them, and re-layouts  186 us (15%)
  starting transfers between devices  104 us (8%)
  matrix products  58.4 us (5%)
  blocking collectives  25.6 us (2%)
    ppermute x64, waiting for transfers between devices, from_behind(): lax.ppermute(shard, axis, [(i, (i + by) % size) for i in range(size)])  510 us
    add x135, other arithmetic, add_tap(): return running + tap_weights[tap_index] * window.astype(jnp.float32)  276 us
    dynamic_slice x135, local copies, waits for them, and re-layouts, add_tap(): return running + tap_weights[tap_index] * window.astype(jnp.float32)  107 us
    ppermute x4, starting transfers between devices, swapped(): lax.ppermute(shard, axis, [(i, i ^ 1 << apart) for i in range(lax.axis_si...  69.2 us
    unnamed x7, other arithmetic  45.2 us
    while x96, local copies, waits for them, and re-layouts  45 us
  transfers between devices with their start and end apart: 71, of which 67 were waited for; matrix products, arithmetic and copies ran while one was open for 5% of the time, Pallas kernels for 0%

commit v1 on v0

v1 whole, which is shorter than its diff:
```python
import math

import jax
import jax.numpy as jnp
from jax import lax
from jax.experimental import pallas as pl
from jax.experimental.pallas import tpu as pltpu
from jax.sharding import PartitionSpec as P

C = 4096
HEAD = 128
EPS = 1e-05
TOK = 128
BLOCKS = 8
SLOT = 144
MESH = pl.DeviceIdType.MESH
F32 = jnp.float32
BF16 = jnp.bfloat16
LIMIT = 60 << 20


def rows_of(step):
    return pl.ds(pl.multiple_of(8 * step, 8), 128)


def front_body(tok_ref, emb_ref, short_ref, med_ref, res_ref, rate_ref, mg_s, yl_s, end_s, lam_s, e_s, sg_s, sw_s, mw_s, cf_s):
    for c in range(BLOCKS):
        lanes = slice(c * 128, (c + 1) * 128)
        sw_s[pl.ds(c, 7, stride=8), :] = short_ref[:, lanes]
        mw_s[pl.ds(c, 128, stride=8), :] = med_ref[:, lanes]
        lam_s[pl.ds(c, 16, stride=8), :] = rate_ref[:, lanes]
        cf_s[pl.ds(c, 16, stride=8), :] = res_ref[:, lanes]
    rate = lam_s[...]
    twice = 2.0 * rate
    tail = jnp.ones_like(twice)
    for k in range(9, 1, -1):
        tail = 1.0 - twice * (1.0 / k) * tail
    cf_s[...] = cf_s[...] * jnp.sqrt(twice * tail) * 0.25
    lam_s[...] = jnp.exp(-rate)

    columns = []
    for k in range(3):
        row = tok_ref[k : k + 1, :].astype(F32)
        columns.append(jnp.broadcast_to(row, (128, 128)).T)
    column = jnp.concatenate([columns[0][112:], columns[1], columns[2]], axis=0)
    lane = lax.broadcasted_iota(jnp.int32, column.shape, 1).astype(F32)
    one_hot = jnp.concatenate(
        [jnp.where(column == lane + 128.0 * k, 1.0, 0.0).astype(BF16) for k in range(4)], axis=1
    )
    for pair in range(4):
        part = jnp.dot(one_hot, emb_ref[:, pair * 256 : pair * 256 + 256], preferred_element_type=F32)
        for k in range(2):
            e_s[pl.ds(2 * pair + k, 272, stride=8), :] = part[:, k * 128 : k * 128 + 128]

    def short_block(block, _):
        first = 16 + block * 16
        own = e_s[rows_of(first), :].reshape(16, 8, 128)
        total = own * sw_s[0:8, :]
        for j in range(1, 7):
            total = total + e_s[rows_of(first - j), :].reshape(16, 8, 128) * sw_s[8 * j : 8 * j + 8, :]
        gated = (own * total).astype(BF16).astype(F32)
        sg_s[rows_of(16 * block), :] = gated.reshape(128, 128)
        return 0

    lax.fori_loop(0, 16, short_block, 0)

    def medium_block(block, _):
        def taps(chunk, total):
            base = 128 + 16 * block - 16 * chunk - 15
            window = sg_s[pl.ds(pl.multiple_of(8 * base, 8), 31 * 8), :].reshape(31, 8, 128)
            weight = mw_s[rows_of(16 * chunk), :].reshape(16, 8, 128)
            for j in range(16):
                total = total + weight[j][None] * window[15 - j : 31 - j]
            return total

        total = lax.fori_loop(0, 8, taps, jnp.zeros((16, 8, 128), F32))
        own = sg_s[rows_of(128 + 16 * block), :].reshape(16, 8, 128)
        gated = (own * total).astype(BF16).astype(F32)
        mg_s[rows_of(16 * block), :] = gated.reshape(128, 128)
        return 0

    lax.fori_loop(0, 8, medium_block, 0)

    lam = lam_s[...].reshape(16, 8, 128)
    coef = cf_s[...].reshape(16, 8, 128)

    def step(block, state):
        for k in range(4):
            tile = pl.ds(pl.multiple_of(8 * (4 * block + k), 8), 8)
            state = lam * state + coef * mg_s[tile, :][None]
            yl_s[tile, :] = jnp.sum(state, axis=0)
        return state

    state = lax.fori_loop(0, 32, step, jnp.zeros((16, 8, 128), F32))
    for r in range(16):
        end_s[pl.ds(r, 8, stride=16), :] = state[r]


def front_kernel(*refs):
    front_body(*refs)


def here():
    seq = lax.axis_index("seq")
    return seq, seq // 8, lax.rem(seq, 8)


def remote(source, target, send, receive, **where):
    return pltpu.make_async_remote_copy(
        src_ref=source, dst_ref=target, send_sem=send, recv_sem=receive, device_id=where, device_id_type=MESH
    )


def greet(names):
    barrier = pltpu.get_barrier_semaphore()
    for where in names:
        pl.semaphore_signal(barrier, inc=1, device_id=where, device_id_type=MESH)
    pl.semaphore_wait(barrier, len(names))


def middle_body(
    rate_ref, mg_s, yl_s, end_s, lam_s, hy_ref, xf_ref,
    got1, got2, got3, pre_s, group_s, h_s, xt_s, inv_s, ss_s,
    send1, recv1, send2, recv2, send3, recv3, sendc, recvc, senda, sendi, recvi, sendx, sends, recvx,
):
    seq, g, i = here()
    ch = lax.axis_index("ch")
    mine = [pl.ds(pl.multiple_of(16 * k, 16), 16) for k in range(8)]

    def part(k):
        return pl.ds(pl.multiple_of(16 * k, 16), 16)

    scans = []
    for d in range(1, 8):
        k = lax.rem(i + d, 8)
        copy = remote(end_s.at[part(k), :], got1.at[part(i), :], send1.at[d], recv1.at[d], seq=8 * g + k)
        copy.start()
        scans.append(copy)
    got1[part(i), :] = end_s[part(i), :]
    rate = rate_ref[:, pl.ds(pl.multiple_of(128 * i, 128), 128)]
    block_decay = jnp.exp(-128.0 * rate)
    group_decay = jnp.exp(-1024.0 * rate)
    for copy in scans:
        copy.wait()
    running = jnp.zeros((16, 128), F32)
    for k in range(8):
        pre_s[16 * k : 16 * k + 16, :] = running
        running = block_decay * running + got1[16 * k : 16 * k + 16, :]
    group_s[...] = running
    scans = []
    for d in range(1, 8):
        k = lax.rem(g + d, 8)
        copy = remote(group_s, got2.at[part(g), :], send2.at[d], recv2.at[d], seq=8 * k + i)
        copy.start()
        scans.append(copy)
    got2[part(g), :] = running
    for copy in scans:
        copy.wait()
    before = jnp.zeros((16, 128), F32)
    for k in range(8):
        before = jnp.where(k < g, group_decay * before + got2[16 * k : 16 * k + 16, :], before)
    for k in range(8):
        pre_s[16 * k : 16 * k + 16, :] = pre_s[16 * k : 16 * k + 16, :] + before
        before = before * block_decay
    scans = []
    for d in range(1, 8):
        k = lax.rem(i + d, 8)
        copy = remote(pre_s.at[part(k), :], got3.at[part(i), :], send3.at[d], recv3.at[d], seq=8 * g + k)
        copy.start()
        scans.append(copy)
    got3[part(i), :] = pre_s[part(i), :]
    for copy in scans:
        copy.wait()

    lam = lam_s[...].reshape(16, 8, 128)
    state = jnp.stack([got3[pl.ds(r, 8, stride=16), :] for r in range(16)], axis=0)

    def step(block, state):
        for k in range(4):
            tile = pl.ds(pl.multiple_of(8 * (4 * block + k), 8), 8)
            state = lam * state
            full = yl_s[tile, :] + jnp.sum(state, axis=0)
            h_s[tile, :] = (mg_s[tile, :] * full).astype(BF16).astype(F32)
        return state

    lax.fori_loop(0, 32, step, state)

    squares = jnp.zeros((128, 128), F32)
    for c in range(BLOCKS):
        block = h_s[pl.ds(c, 128, stride=8), :]
        hy_ref[:, c * 128 : (c + 1) * 128] = block.astype(BF16)
        turned = block.T
        xt_s[c] = turned.astype(BF16)
        squares = squares + turned * turned
    ss_s[ch] = jnp.broadcast_to(jnp.sum(squares, axis=0, keepdims=True), (8, 128))

    chans = []
    for d in range(1, 4):
        k = lax.rem(ch + d, 4)
        copy = remote(ss_s.at[ch], ss_s.at[ch], sendc.at[d], recvc.at[d], ch=k)
        copy.start()
        chans.append(copy)
    slot = 8 * g + i
    blocks = []
    for d in range(1, 8):
        k = lax.rem(g + d, 8)
        copy = remote(
            xt_s.at[k], xf_ref.at[slot, pl.ds(0, 128), :], senda.at[d], recvx.at[slot], seq=8 * k + i
        )
        copy.start()
        blocks.append(copy)
    xf_ref[slot, 0:128, :] = xt_s[g]
    for copy in chans:
        copy.wait()
    sums = ss_s[0] + ss_s[1] + ss_s[2] + ss_s[3]
    scale = lax.rsqrt(sums / C + EPS)
    high = scale.astype(BF16).astype(F32)
    middle = (scale - high).astype(BF16).astype(F32)
    low = scale - high - middle
    index = lax.broadcasted_iota(jnp.int32, (8, 128), 0)
    packed = jnp.where(index == 0, high, jnp.where(index == 1, middle, low))
    inv_s[...] = jnp.concatenate([packed, jnp.zeros((8, 128), F32)], axis=0).astype(BF16)
    scales = []
    for d in range(1, 8):
        k = lax.rem(g + d, 8)
        copy = remote(
            inv_s, xf_ref.at[slot, pl.ds(128, 16), :], sendi.at[d], recvi.at[d], seq=8 * k + i
        )
        copy.start()
        scales.append(copy)
    xf_ref[slot, 128:144, :] = inv_s[...]

    core = lax.rem(i, 2)
    x = i // 2
    other = 8 * g + 2 * x + 1 - core

    def arrival(b, rows):
        return pltpu.make_async_copy(xf_ref.at[b, rows, :], xf_ref.at[b, rows, :], recvx.at[b])

    passed = []
    for d in range(8):
        k = lax.rem(g + 8 - d, 8)
        b = 8 * k + i
        if d:
            arrival(b, pl.ds(0, 128)).wait()
            scales[d - 1].wait_recv()
        for s in range(1, 4):
            to = 8 * g + 2 * lax.rem(x + s, 4) + core
            copy = remote(xf_ref.at[b], xf_ref.at[b], sendx.at[3 * d + s - 1], recvx.at[b], seq=to)
            copy.start()
            passed.append(copy)
        copy = remote(xf_ref.at[b], xf_ref.at[b], sends.at[4 * d], recvx.at[b], seq=other)
        copy.start()
        passed.append(copy)
    for d in range(8):
        k = lax.rem(g + 8 - d, 8)
        for s in range(1, 4):
            b = 8 * k + 2 * lax.rem(x + 4 - s, 4) + core
            arrival(b, pl.ds(0, SLOT)).wait()
            copy = remote(xf_ref.at[b], xf_ref.at[b], sends.at[4 * d + s], recvx.at[b], seq=other)
            copy.start()
            passed.append(copy)
    for d in range(8):
        k = lax.rem(g + 8 - d, 8)
        for s in range(4):
            b = 8 * k + 2 * lax.rem(x + 4 - s, 4) + 1 - core
            arrival(b, pl.ds(0, SLOT)).wait()
    for copy in blocks + scales + passed:
        copy.wait_send()


def middle_kernel(*refs):
    seq, g, i = here()
    ch = lax.axis_index("ch")
    names = [{"seq": 8 * g + lax.rem(i + d, 8)} for d in range(1, 8)]
    names += [{"seq": 8 * lax.rem(g + d, 8) + i} for d in range(1, 8)]
    names += [{"ch": lax.rem(ch + d, 4)} for d in range(1, 4)]
    greet(names)
    middle_body(*refs)


def attend_body(xf_ref, qg_ref, kg_ref, o_ref, kt_s, vt_s, q_s):
    seq, g, i = here()
    query_gain = qg_ref[pl.ds(g, 1), :]
    key_gain = jnp.broadcast_to(kg_ref[pl.ds(g, 1), :], (128, 128)).T

    def normed(b):
        scale = xf_ref[b, 128:144, :].astype(F32)
        scale = scale[0:1] + (scale[1:2] + scale[2:3])
        return xf_ref[b, 0:128, :].astype(F32) * scale

    def prepare(segment, _):
        for k in range(8):
            rows = normed(8 * segment + k)
            vt_s[segment, :, k * 128 : (k + 1) * 128] = rows.astype(BF16)
            kt_s[segment, :, k * 128 : (k + 1) * 128] = (rows * key_gain).astype(BF16)
        q_s[segment] = (normed(8 * segment + i).T * query_gain).astype(BF16)
        return 0

    lax.fori_loop(0, 8, prepare, 0)
    factor = HEAD ** (-0.5) * math.log2(math.e)
    row = lax.broadcasted_iota(jnp.int32, (128, 1024), 0) + 128 * i
    allowed = lax.broadcasted_iota(jnp.int32, (128, 1024), 1) <= row

    for n in range(8):
        query = q_s[n]

        def tile(segment, carry, diagonal):
            peak, total, blend = carry
            score = jnp.dot(query, kt_s[segment], preferred_element_type=F32) * factor
            if diagonal:
                score = jnp.where(allowed, score, -1e30)
            new_peak = jnp.maximum(peak, jnp.max(score, axis=1, keepdims=True))
            weight = jnp.exp2(score - new_peak)
            shrink = jnp.exp2(peak - new_peak)
            total = total * shrink + jnp.sum(weight, axis=1, keepdims=True)
            blend = blend * shrink + lax.dot_general(
                weight.astype(BF16), vt_s[segment], (((1,), (1,)), ((), ())), preferred_element_type=F32
            )
            return new_peak, total, blend

        carry = (jnp.full((128, 1), -1e30, F32), jnp.zeros((128, 1), F32), jnp.zeros((128, 128), F32))
        carry = tile(n, carry, True)
        if n:
            carry = lax.fori_loop(0, n, lambda s, carry: tile(s, carry, False), carry)
        o_ref[n] = (carry[2] / carry[1]).astype(BF16)


def return_kernel(o_ref, out_ref, send, recv):
    seq, g, i = here()
    greet([{"seq": 8 * lax.rem(g + d, 8) + i} for d in range(1, 8)])
    mine = pl.ds(pl.multiple_of(128 * g, 128), 128)
    copies = []
    for d in range(1, 8):
        k = lax.rem(g + d, 8)
        copy = remote(o_ref.at[k], out_ref.at[:, mine], send.at[d], recv.at[d], seq=8 * k + i)
        copy.start()
        copies.append(copy)
    out_ref[:, mine] = o_ref[g]
    for copy in copies:
        copy.wait()


def vmem(*shape, dtype=F32):
    return pltpu.VMEM(shape, dtype)


def in_vmem(count):
    return [pl.BlockSpec(memory_space=pltpu.VMEM)] * count


def dmas(count):
    return pltpu.SemaphoreType.DMA((count,))


def on_device(
    token_ids, embedding, short_filter, medium_filter, long_residue, long_rate, query_gain, key_gain
):
    seq_count = lax.axis_size("seq")
    lifted = token_ids + 1
    near = lax.ppermute(lifted, "seq", [(k, k + 1) for k in range(seq_count - 1)])
    far = lax.ppermute(lifted, "seq", [(k, k + 2) for k in range(seq_count - 2)])
    tokens = jnp.stack([far, near, lifted]) - 1

    shape = jax.ShapeDtypeStruct
    gated, local, ends, decay = pl.pallas_call(
        front_kernel,
        out_shape=[shape((1024, 128), F32), shape((1024, 128), F32), shape((128, 128), F32), shape((128, 128), F32)],
        in_specs=in_vmem(6),
        out_specs=in_vmem(4),
        scratch_shapes=[vmem(2176, 128), vmem(2048, 128), vmem(64, 128), vmem(1024, 128), vmem(128, 128)],
        compiler_params=pltpu.CompilerParams(vmem_limit_bytes=LIMIT),
        name="front",
    )(tokens, embedding, short_filter, medium_filter, long_residue, long_rate)

    hyena_out, blocks = pl.pallas_call(
        middle_kernel,
        out_shape=[shape((TOK, 1024), BF16), shape((64, SLOT, 128), BF16)],
        in_specs=in_vmem(5),
        out_specs=in_vmem(2),
        scratch_shapes=[
            vmem(128, 128), vmem(128, 128), vmem(128, 128), vmem(128, 128), vmem(16, 128),
            vmem(1024, 128), vmem(8, 128, 128, dtype=BF16), vmem(16, 128, dtype=BF16), vmem(4, 8, 128),
            dmas(8), dmas(8), dmas(8), dmas(8), dmas(8), dmas(8), dmas(4), dmas(4), dmas(8), dmas(8), dmas(8),
            dmas(24), dmas(32), dmas(64),
        ],
        compiler_params=pltpu.CompilerParams(vmem_limit_bytes=LIMIT, collective_id=0, has_side_effects=True),
        name="middle",
    )(long_rate, gated, local, ends, decay)

    blended = pl.pallas_call(
        attend_body,
        out_shape=shape((8, 128, 128), BF16),
        in_specs=in_vmem(3),
        out_specs=in_vmem(1)[0],
        scratch_shapes=[vmem(8, 128, 1024, dtype=BF16), vmem(8, 128, 1024, dtype=BF16), vmem(8, 128, 128, dtype=BF16)],
        compiler_params=pltpu.CompilerParams(vmem_limit_bytes=LIMIT),
        name="attend",
    )(blocks, query_gain.reshape(8, 128), key_gain.reshape(8, 128))

    attended = pl.pallas_call(
        return_kernel,
        out_shape=shape((TOK, 1024), BF16),
        in_specs=in_vmem(1),
        out_specs=in_vmem(1)[0],
        scratch_shapes=[dmas(8), dmas(8)],
        compiler_params=pltpu.CompilerParams(vmem_limit_bytes=LIMIT, collective_id=1, has_side_effects=True),
        name="give_back",
    )(blended)
    return hyena_out, attended


def solution(mesh):
    in_specs = (
        P("seq"),
        P(None, "ch"),
        P(None, "ch"),
        P(None, "ch"),
        P(None, "ch"),
        P(None, "ch"),
        P("ch"),
        P("ch"),
    )
    out_specs = (P("seq", "ch"), P("seq", "ch"))
    return jax.shard_map(
        on_device, mesh=mesh, in_specs=in_specs, out_specs=out_specs, check_vma=False
    )
```

time: 1270 us -> 118 us (0.09)
  the two profiles are of different devices: /device:TPU:175 before, /device:TPU:1 now
where the time goes in v1:
time: 118 us; the launch traced here: 117 us
  Pallas kernels  104 us (88%)
  starting transfers between devices  7.61 us (6%)
  local copies, waits for them, and re-layouts  2.38 us (2%)
  other arithmetic  1.26 us (1%)
    pallas_call x1, Pallas kernels, on_device(): pl.pallas_call(middle_kernel, out_shape=[shape((TOK, 1024), BF16), shape(...  57.6 us
    pallas_call x1, Pallas kernels, on_device(): pl.pallas_call(attend_body, out_shape=shape((8, 128, 128), BF16), in_spec...  22.4 us
    pallas_call x1, Pallas kernels, on_device(): pl.pallas_call(return_kernel, out_shape=shape((TOK, 1024), BF16), in_spec...  13.8 us
    pallas_call x1, Pallas kernels, on_device(): pl.pallas_call(front_kernel, out_shape=[shape((1024, 128), F32), shape((1...  10.3 us
    ppermute x1, starting transfers between devices, on_device(): lax.ppermute(lifted, 'seq', [(k, k + 1) for k in range(seq_count - 1)])  4.5 us
    ppermute x1, starting transfers between devices, on_device(): lax.ppermute(lifted, 'seq', [(k, k + 2) for k in range(seq_count - 2)])  3.12 us
    unnamed x4, local copies, waits for them, and re-layouts  2.38 us
  transfers between devices with their start and end apart: 2, of which 1 were waited for; matrix products, arithmetic and copies ran while one was open for 0% of the time, Pallas kernels for 0%

profile of v1, /device:TPU:1, one launch (start us, length us, event | category | flops | bytes accessed | tf_op | source)
XLA Modules:
  0.0 116.8 jit_solution(7776892814760416131)
XLA Ops:
  0.6 0.7 broadcast_add_fusion
  1.3 4.5 %collective-permute-start.1 = (s32[128]{0:T(128)S(1)}, s32[128]{0:T(128)S(1)}, u32[]{:S(2)}, u32[]{:S(2)}) collective-permute-start(s32[128]{0:T(128)S(1)} %get-tuple-element.14), channel_id=1, source_target_pairs={{0,4},{4,8},{8,12},{12,16},{16,20},{20,24},{24,28},{28,32},{32,36}... | collective-permute-start | bytes 1544 | tf_op jit(solution)/shard_map/ppermute | solution.py:361
  5.8 3.1 %collective-permute-start = (s32[128]{0:T(128)S(1)}, s32[128]{0:T(128)S(1)}, u32[]{:S(2)}, u32[]{:S(2)}) collective-permute-start(s32[128]{0:T(128)S(1)} %get-tuple-element.14), channel_id=1, source_target_pairs={{0,8},{4,12},{8,16},{12,20},{16,24},{20,28},{24,32},{28,36},{32,40... | collective-permute-start | bytes 1544 | tf_op jit(solution)/shard_map/ppermute | solution.py:362
  8.9 0.0 collective-permute-done.1
  8.9 0.7 collective-permute-done
  9.6 0.6 add_add_fusion.refs_0_
  10.2 10.3 %front.1 = (f32[1024,128]{1,0:T(8,128)}, f32[1024,128]{1,0:T(8,128)}, f32[128,128]{1,0:T(8,128)}, f32[128,128]{1,0:T(8,128)}) custom-call(s32[3,128]{1,0:T(4,128)} %add_add_fusion.refs_0_, bf16[512,1024]{1,0:T(8,128)(2,1)} %refs_1_.1, f32[7,1024]{1,0:T(8,128)} %refs_2_.1, f32[128,1024]{1,0:T(8,128)} %refs_3_.1, f32[16,1024]{1,0:T(8,128)} %refs_4_.1, ...), custom_call_target="tpu_custom_call" | custom-call | tf_op jit(solution)/shard_map/front/pallas_call | solution.py:366
  20.5 57.6 %middle.1 = (bf16[128,1024]{1,0:T(8,128)(2,1)}, bf16[64,144,128]{2,1,0:T(8,128)(2,1)}) custom-call(f32[16,1024]{1,0:T(8,128)} %refs_0_.1, f32[1024,128]{1,0:T(8,128)} %get-tuple-element.8.refs_1_, f32[1024,128]{1,0:T(8,128)} %get-tuple-element.9.refs_2_, f32[128,128]{1,0:T(8,128)} %get-tuple-element.10.refs_3_, f32[128,128]{1,0:T(8,128)} %get-tuple-element.11.refs_4_), custom_call_target="tpu_custom_call" | custom-call | tf_op jit(solution)/shard_map/middle/pallas_call | solution.py:376
  78.1 0.0 copy-start
  78.2 22.4 %attend.1.o_ref = bf16[8,128,128]{2,1,0:T(8,128)(2,1)} custom-call(bf16[64,144,128]{2,1,0:T(8,128)(2,1)} %get-tuple-element.13.xf_ref, f32[8,128]{1,0:T(8,128)} %bitcast.6, f32[8,128]{1,0:T(8,128)} %bitcast.7), custom_call_target="tpu_custom_call" | custom-call | tf_op jit(solution)/shard_map/attend/pallas_call | solution.py:391
  100.5 13.8 %give_back.1 = bf16[128,1024]{1,0:T(8,128)(2,1)} custom-call(bf16[8,128,128]{2,1,0:T(8,128)(2,1)} %attend.1.o_ref), custom_call_target="tpu_custom_call" | custom-call | tf_op jit(solution)/shard_map/give_back/pallas_call | solution.py:401
  114.4 0.0 copy-done
  114.4 0.7 copy.12
  115.1 1.7 %copy.13 = bf16[128,1024]{1,0:T(8,128)(2,1)} copy(bf16[128,1024]{1,0:T(8,128)(2,1)} %give_back.1) | data formatting | bytes 524288
Async XLA Ops:
  1.3 7.6 %collective-permute-start.1 = (s32[128]{0:T(128)S(1)}, s32[128]{0:T(128)S(1)}, u32[]{:S(2)}, u32[]{:S(2)}) collective-permute-start(s32[128]{0:T(128)S(1)} %get-tuple-element.14), channel_id=1, source_target_pairs={{0,4},{4,8},{8,12},{12,16},{16,20},{20,24},{24,28},{28,32},{32,36}... | collective-permute-start | bytes 1544 | tf_op jit(solution)/shard_map/ppermute | solution.py:361
  5.8 3.8 %collective-permute-start = (s32[128]{0:T(128)S(1)}, s32[128]{0:T(128)S(1)}, u32[]{:S(2)}, u32[]{:S(2)}) collective-permute-start(s32[128]{0:T(128)S(1)} %get-tuple-element.14), channel_id=1, source_target_pairs={{0,8},{4,12},{8,16},{12,20},{16,24},{20,28},{24,32},{28,36},{32,40... | collective-permute-start | bytes 1544 | tf_op jit(solution)/shard_map/ppermute | solution.py:362
  78.1 36.2 %copy-start = (bf16[128,1024]{1,0:T(8,128)(2,1)S(1)}, bf16[128,1024]{1,0:T(8,128)(2,1)}, u32[]{:S(2)}) copy-start(bf16[128,1024]{1,0:T(8,128)(2,1)} %get-tuple-element.18) | copy-start | bytes 786436

commit v2 on v1

v2 whole, which is shorter than its diff:
```python
import math

import jax
import jax.numpy as jnp
from jax import lax
from jax.experimental import pallas as pl
from jax.experimental.pallas import tpu as pltpu
from jax.sharding import PartitionSpec as P

C = 4096
HEAD = 128
EPS = 1e-05
TOK = 128
BLOCKS = 8
MESH = pl.DeviceIdType.MESH
F32 = jnp.float32
BF16 = jnp.bfloat16
LIMIT = 60 << 20

OFFSETS = ((0, 0), (1, 0), (3, 0), (2, 0), (0, 1), (1, 1), (3, 1), (2, 1))


def rows_of(step):
    return pl.ds(pl.multiple_of(8 * step, 8), 128)


def part(k):
    return pl.ds(pl.multiple_of(16 * k, 16), 16)


def here():
    seq = lax.axis_index("seq")
    return seq, seq // 8, lax.rem(seq, 8)


def remote(source, target, send, receive, **where):
    return pltpu.make_async_remote_copy(
        src_ref=source, dst_ref=target, send_sem=send, recv_sem=receive, device_id=where, device_id_type=MESH
    )


def landed(ref, semaphore):
    pltpu.make_async_copy(ref, ref, semaphore).wait()


def embed(tokens, emb_ref, e_s, first, keep):
    column = jnp.broadcast_to(tokens.astype(F32), (128, 128)).T[128 - keep :]
    lane = lax.broadcasted_iota(jnp.int32, column.shape, 1).astype(F32)
    one_hot = jnp.concatenate(
        [jnp.where(column == lane + 128.0 * k, 1.0, 0.0).astype(BF16) for k in range(4)], axis=1
    )
    for pair in range(4):
        rows = jnp.dot(one_hot, emb_ref[:, pair * 256 : pair * 256 + 256], preferred_element_type=F32)
        for k in range(2):
            e_s[pl.ds(8 * first + 2 * pair + k, keep, stride=8), :] = rows[:, k * 128 : k * 128 + 128]


def whole_kernel(
    tok_ref, emb_ref, short_ref, med_ref, res_ref, rate_ref, qg_ref, kg_ref, hy_ref, out_ref,
    near_s, far_s, e_s, sg_s, sw_s, mw_s, cf_s, lam_s, mg_s, yl_s, end_s,
    got1, got2, got3, pre_s, group_s, h_s, xt_s, ss_s, inv_s, xf_s, kn_s, vt_s, q_s, o_s,
    sendt, recvt, send1, recv1, send2, recv2, send3, recv3, sendc, recvc, sendi, recvi, sendj, recvj,
    senda, sendx, sendo, recvx, sendr, recvr,
):
    seq, g, i = here()
    ch = lax.axis_index("ch")
    y, half, x, core = g // 2, lax.rem(g, 2), i // 2, lax.rem(i, 2)

    def group_at(dy, dz):
        return 2 * lax.rem(y + dy, 4) + lax.rem(half + dz, 2)

    names = [{"seq": 8 * g + lax.rem(i + d, 8)} for d in range(1, 8)]
    names += [{"seq": 8 * lax.rem(g + d, 8) + i} for d in range(1, 8)]
    names += [{"ch": lax.rem(ch + d, 4)} for d in range(1, 4)]
    names += [{"seq": lax.rem(seq + d, 64)} for d in (1, 2, 62, 63)]
    barrier = pltpu.get_barrier_semaphore()
    for where in names:
        pl.semaphore_signal(barrier, inc=1, device_id=where, device_id_type=MESH)

    for c in range(BLOCKS):
        lanes = slice(c * 128, (c + 1) * 128)
        sw_s[pl.ds(c, 7, stride=8), :] = short_ref[:, lanes]
        mw_s[pl.ds(c, 128, stride=8), :] = med_ref[:, lanes]
        lam_s[pl.ds(c, 16, stride=8), :] = rate_ref[:, lanes]
        cf_s[pl.ds(c, 16, stride=8), :] = res_ref[:, lanes]
    rate = lam_s[...]
    twice = 2.0 * rate
    tail = jnp.ones_like(twice)
    for k in range(9, 1, -1):
        tail = 1.0 - twice * (1.0 / k) * tail
    cf_s[...] = cf_s[...] * jnp.sqrt(twice * tail) * 0.25
    lam_s[...] = jnp.exp(-rate)
    embed(tok_ref[...], emb_ref, e_s, 144, 128)

    pl.semaphore_wait(barrier, len(names))
    tokens = [
        remote(tok_ref, near_s, sendt.at[0], recvt.at[0], seq=lax.rem(seq + 1, 64)),
        remote(tok_ref, far_s, sendt.at[1], recvt.at[1], seq=lax.rem(seq + 2, 64)),
    ]
    for copy in tokens:
        copy.start()

    def short_block(block, _):
        first = 16 + block * 16
        own = e_s[rows_of(first), :].reshape(16, 8, 128)
        total = own * sw_s[0:8, :]
        for j in range(1, 7):
            total = total + e_s[rows_of(first - j), :].reshape(16, 8, 128) * sw_s[8 * j : 8 * j + 8, :]
        gated = (own * total).astype(BF16).astype(F32)
        sg_s[rows_of(16 * block), :] = gated.reshape(128, 128)
        return 0

    lax.fori_loop(9, 16, short_block, 0)
    for copy in tokens:
        copy.wait()
    embed(jnp.where(seq >= 1, near_s[...], -1), emb_ref, e_s, 16, 128)
    embed(jnp.where(seq >= 2, far_s[...], -1), emb_ref, e_s, 0, 16)
    lax.fori_loop(0, 9, short_block, 0)

    def medium_block(block, _):
        def taps(chunk, total):
            base = 128 + 16 * block - 16 * chunk - 15
            window = sg_s[pl.ds(pl.multiple_of(8 * base, 8), 31 * 8), :].reshape(31, 8, 128)
            weight = mw_s[rows_of(16 * chunk), :].reshape(16, 8, 128)
            for j in range(16):
                total = total + weight[j][None] * window[15 - j : 31 - j]
            return total

        total = lax.fori_loop(0, 8, taps, jnp.zeros((16, 8, 128), F32))
        own = sg_s[rows_of(128 + 16 * block), :].reshape(16, 8, 128)
        gated = (own * total).astype(BF16).astype(F32)
        mg_s[rows_of(16 * block), :] = gated.reshape(128, 128)
        return 0

    lax.fori_loop(0, 8, medium_block, 0)

    lam = lam_s[...].reshape(16, 8, 128)
    coef = cf_s[...].reshape(16, 8, 128)

    def tile_of(step):
        return pl.ds(pl.multiple_of(8 * step, 8), 8)

    def forget(block, state):
        for k in range(8):
            state = lam * state + coef * mg_s[tile_of(8 * block + k), :][None]
        return state

    state = lax.fori_loop(0, 16, forget, jnp.zeros((16, 8, 128), F32))
    for r in range(16):
        end_s[pl.ds(r, 8, stride=16), :] = state[r]

    first_scan, second_scan, third_scan = [], [], []
    for d in range(1, 8):
        k = lax.rem(i + d, 8)
        copy = remote(end_s.at[part(k), :], got1.at[part(i), :], send1.at[d], recv1.at[d], seq=8 * g + k)
        copy.start()
        first_scan.append(copy)
    got1[part(i), :] = end_s[part(i), :]

    def local(block, state):
        for k in range(4):
            tile = tile_of(4 * block + k)
            state = lam * state + coef * mg_s[tile, :][None]
            yl_s[tile, :] = jnp.sum(state, axis=0)
        return state

    lax.fori_loop(0, 32, local, jnp.zeros((16, 8, 128), F32))
    rate = rate_ref[:, pl.ds(pl.multiple_of(128 * i, 128), 128)]
    block_decay = jnp.exp(-128.0 * rate)
    group_decay = jnp.exp(-1024.0 * rate)
    for copy in first_scan:
        copy.wait()
    running = jnp.zeros((16, 128), F32)
    for k in range(8):
        pre_s[16 * k : 16 * k + 16, :] = running
        running = block_decay * running + got1[16 * k : 16 * k + 16, :]
    group_s[...] = running
    for d in range(7, 0, -1):
        k = group_at(*OFFSETS[d])
        copy = remote(group_s, got2.at[part(g), :], send2.at[d], recv2.at[d], seq=8 * k + i)
        copy.start()
        second_scan.append(copy)
    got2[part(g), :] = running
    for copy in second_scan:
        copy.wait()
    before = jnp.zeros((16, 128), F32)
    for k in range(8):
        before = jnp.where(k < g, group_decay * before + got2[16 * k : 16 * k + 16, :], before)
    for k in range(8):
        pre_s[16 * k : 16 * k + 16, :] = pre_s[16 * k : 16 * k + 16, :] + before
        before = before * block_decay
    for d in range(1, 8):
        k = lax.rem(i + d, 8)
        copy = remote(pre_s.at[part(k), :], got3.at[part(i), :], send3.at[d], recv3.at[d], seq=8 * g + k)
        copy.start()
        third_scan.append(copy)
    got3[part(i), :] = pre_s[part(i), :]
    for copy in third_scan:
        copy.wait()

    state = jnp.stack([got3[pl.ds(r, 8, stride=16), :] for r in range(16)], axis=0)

    def carried(block, state):
        for k in range(4):
            tile = tile_of(4 * block + k)
            state = lam * state
            full = yl_s[tile, :] + jnp.sum(state, axis=0)
            h_s[tile, :] = (mg_s[tile, :] * full).astype(BF16).astype(F32)
        return state

    lax.fori_loop(0, 32, carried, state)

    squares = jnp.zeros((128, 128), F32)
    for c in range(BLOCKS):
        block = h_s[pl.ds(c, 128, stride=8), :]
        turned = block.T
        xt_s[c] = turned.astype(BF16)
        squares = squares + turned * turned
        hy_ref[:, c * 128 : (c + 1) * 128] = block.astype(BF16)
    ss_s[ch] = jnp.sum(squares, axis=0, keepdims=True)

    sums = []
    for d in range(1, 4):
        k = lax.rem(ch + d, 4)
        copy = remote(ss_s.at[ch], ss_s.at[ch], sendc.at[d], recvc.at[d], ch=k)
        copy.start()
        sums.append(copy)
    slot = 8 * g + i
    sent = []
    for d in range(7, 0, -1):
        k = group_at(*OFFSETS[d])
        copy = remote(xt_s.at[k], xf_s.at[slot], senda.at[d], recvx.at[slot], seq=8 * k + i)
        copy.start()
        sent.append(copy)
    xf_s[slot] = xt_s[g]

    sources = [2 * lax.rem(y + 4 - dy, 4) + lax.rem(half + dz, 2) for dy, dz in OFFSETS]
    places = [8 * k for k in sources]
    right, left = 8 * g + 2 * lax.rem(x + 1, 4) + core, 8 * g + 2 * lax.rem(x + 3, 4) + core
    other = 8 * g + 2 * x + 1 - core

    def along(b, n, semaphores, to):
        copy = remote(xf_s.at[b], xf_s.at[b], semaphores.at[n], recvx.at[b], seq=to)
        copy.start()
        sent.append(copy)

    def own_column(d):
        b = places[d] + i
        if d:
            landed(xf_s.at[b], recvx.at[b])
        along(b, 3 * d, sendx, right)
        along(b, 3 * d + 1, sendx, left)
        along(b, 4 * d, sendo, other)

    def neighbours(d):
        b = places[d] + 2 * lax.rem(x + 3, 4) + core
        landed(xf_s.at[b], recvx.at[b])
        if d % 2 == 0:
            along(b, 3 * d + 2, sendx, right)
        along(b, 4 * d + 1, sendo, other)
        b = places[d] + 2 * lax.rem(x + 1, 4) + core
        landed(xf_s.at[b], recvx.at[b])
        if d % 2 == 1:
            along(b, 3 * d + 2, sendx, left)
        along(b, 4 * d + 2, sendo, other)

    def opposite(d):
        b = places[d] + 2 * lax.rem(x + 2, 4) + core
        landed(xf_s.at[b], recvx.at[b])
        along(b, 4 * d + 3, sendo, other)

    def row_at(i_, g_):
        return 8 * i_ + 4 * lax.rem(g_, 2) + g_ // 2

    def scales_out(z):
        rows = pl.ds(8 * i + 4 * lax.rem(half + z, 2), 4)
        for d in range(4 * z, 4 * z + 4):
            if d:
                landed(inv_s.at[row_at(i, sources[d])], recvi.at[d])
        for d in range(1, 8):
            to = 8 * g + lax.rem(i + d, 8)
            copy = remote(inv_s.at[rows], inv_s.at[rows], sendj.at[8 * z + d], recvj.at[8 * z + d], seq=to)
            copy.start()
            sent.append(copy)

    def scales_in(z):
        for d in range(1, 8):
            rows = pl.ds(8 * lax.rem(i + 8 - d, 8) + 4 * lax.rem(half + z, 2), 4)
            landed(inv_s.at[rows], recvj.at[8 * z + d])

    query_gain = jnp.broadcast_to(qg_ref[pl.ds(g, 1), :], (128, 128)).T
    key_gain = jnp.broadcast_to(kg_ref[pl.ds(g, 1), :], (128, 128)).T

    def normed(b, i_, g_):
        return xf_s[b].astype(F32) * inv_s[row_at(i_, g_)]

    def prepare(d):
        k = sources[d]
        for s in range(4):
            b = places[d] + 2 * lax.rem(x + s, 4) + 1 - core
            landed(xf_s.at[b], recvx.at[b])
        for n in range(8):
            rows = normed(places[d] + n, n, k)
            vt_s[k, :, 128 * n : 128 * n + 128] = rows.astype(BF16)
            kn_s[k, 128 * n : 128 * n + 128, :] = (rows * key_gain).T.astype(BF16)

    own_column(0)
    for copy in sums:
        copy.wait()
    total = ss_s[0] + ss_s[1] + ss_s[2] + ss_s[3]
    inv_s[row_at(i, g)] = lax.rsqrt(total / C + EPS)
    mine = inv_s.at[row_at(i, g)]
    for d in range(7, 0, -1):
        copy = remote(mine, mine, sendi.at[d], recvi.at[d], seq=8 * group_at(*OFFSETS[d]) + i)
        copy.start()
        sent.append(copy)
    own_column(1)
    own_column(2)
    neighbours(0)
    own_column(3)
    neighbours(1)
    opposite(0)
    scales_out(0)
    neighbours(2)
    opposite(1)
    neighbours(3)
    own_column(4)
    opposite(2)
    own_column(5)
    neighbours(4)
    opposite(3)
    own_column(6)
    neighbours(5)
    own_column(7)
    scales_out(1)
    opposite(4)
    neighbours(6)
    scales_in(0)
    prepare(0)
    opposite(5)
    neighbours(7)
    prepare(1)
    opposite(6)
    prepare(2)
    opposite(7)
    prepare(3)
    for n in range(8):
        q_s[:, 128 * n : 128 * n + 128] = (normed(8 * n + i, i, n) * query_gain).astype(BF16)
    scales_in(1)
    for d in range(4, 8):
        prepare(d)

    factor = HEAD ** (-0.5) * math.log2(math.e)
    column = lax.broadcasted_iota(jnp.int32, (1024, 128), 1) + 128 * i
    allowed = lax.broadcasted_iota(jnp.int32, (1024, 128), 0) <= column

    def attend(n, segment, carry, diagonal):
        peak, total, blend = carry
        score = jnp.dot(kn_s[segment], q_s[:, 128 * n : 128 * n + 128], preferred_element_type=F32) * factor
        if diagonal:
            score = jnp.where(allowed, score, -1e30)
        new_peak = jnp.maximum(peak, jnp.max(score, axis=0, keepdims=True))
        weight = jnp.exp2(score - new_peak)
        shrink = jnp.exp2(peak - new_peak)
        total = total * shrink + jnp.sum(weight, axis=0, keepdims=True)
        blend = blend * shrink + jnp.dot(vt_s[segment], weight.astype(BF16), preferred_element_type=F32)
        return new_peak, total, blend

    columns = pl.ds(pl.multiple_of(128 * g, 128), 128)
    given = [
        remote(o_s.at[n], out_ref.at[:, columns], sendr.at[n], recvr.at[g], seq=8 * n + i) for n in range(8)
    ]
    for base in (4, 0):
        carries = [
            (jnp.full((1, 128), -1e30, F32), jnp.zeros((1, 128), F32), jnp.zeros((128, 128), F32))
            for _ in range(4)
        ]
        for segment in range(base, base + 4):
            for n in range(segment, base + 4):
                carries[n - base] = attend(n, segment, carries[n - base], n == segment)
        if base:
            carries = lax.fori_loop(
                0, base, lambda s, held: [attend(base + n, s, held[n], False) for n in range(4)], carries
            )
        for n in range(4):
            o_s[base + n] = (carries[n][2] / carries[n][1]).T.astype(BF16)
        for n in range(base, base + 4):
            pl.when(g != n)(given[n].start)
    out_ref[:, columns] = o_s[g]
    for n in range(8):

        @pl.when(g != n)
        def _(n=n):
            landed(out_ref.at[:, pl.ds(128 * n, 128)], recvr.at[n])
            given[n].wait_send()

    for copy in sent:
        copy.wait_send()


def vmem(*shape, dtype=F32):
    return pltpu.VMEM(shape, dtype)


def in_vmem(count):
    return [pl.BlockSpec(memory_space=pltpu.VMEM)] * count


def dmas(count):
    return pltpu.SemaphoreType.DMA((count,))


def on_device(
    token_ids, embedding, short_filter, medium_filter, long_residue, long_rate, query_gain, key_gain
):
    shape = jax.ShapeDtypeStruct
    counts = (2, 2, 8, 8, 8, 8, 8, 8, 4, 4, 8, 8, 16, 16, 8, 24, 32, 64, 8, 8)
    return pl.pallas_call(
        whole_kernel,
        out_shape=[shape((TOK, 1024), BF16), shape((TOK, 1024), BF16)],
        in_specs=in_vmem(8),
        out_specs=in_vmem(2),
        scratch_shapes=[
            vmem(1, 128, dtype=jnp.int32), vmem(1, 128, dtype=jnp.int32),
            vmem(2176, 128), vmem(2048, 128), vmem(64, 128), vmem(1024, 128), vmem(128, 128), vmem(128, 128),
            vmem(1024, 128), vmem(1024, 128), vmem(128, 128),
            vmem(128, 128), vmem(128, 128), vmem(128, 128), vmem(128, 128), vmem(16, 128),
            vmem(1024, 128), vmem(8, 128, 128, dtype=BF16), vmem(4, 1, 128), vmem(64, 1, 128),
            vmem(64, 128, 128, dtype=BF16), vmem(8, 1024, 128, dtype=BF16), vmem(8, 128, 1024, dtype=BF16),
            vmem(128, 1024, dtype=BF16), vmem(8, 128, 128, dtype=BF16),
        ]
        + [dmas(count) for count in counts],
        compiler_params=pltpu.CompilerParams(vmem_limit_bytes=LIMIT, collective_id=0, has_side_effects=True),
        name="whole",
    )(
        token_ids.reshape(1, TOK), embedding, short_filter, medium_filter, long_residue, long_rate,
        query_gain.reshape(8, 128), key_gain.reshape(8, 128),
    )


def solution(mesh):
    in_specs = (
        P("seq"),
        P(None, "ch"),
        P(None, "ch"),
        P(None, "ch"),
        P(None, "ch"),
        P(None, "ch"),
        P("ch"),
        P("ch"),
    )
    out_specs = (P("seq", "ch"), P("seq", "ch"))
    return jax.shard_map(
        on_device, mesh=mesh, in_specs=in_specs, out_specs=out_specs, check_vma=False
    )
```

time: 118 us -> 83.6 us (0.71)
  Pallas kernels: 104 us -> 80.4 us
  starting transfers between devices: 7.61 us -> 0 us
  other arithmetic: 1.26 us -> 0 us
    pallas_call x4 -> x1, Pallas kernels: 104 us -> 80.4 us  [on_device(): pl.pallas_call(whole_kernel, out_shape=[shape((TOK, 1024), BF16), shape((...]
    ppermute x2 -> x0, starting transfers between devices: 7.61 us -> none  [the longest x1 4.5 us: on_device(): lax.ppermute(lifted, 'seq', [(k, k + 1) for k in range(seq_count - 1)])]
  transfers between devices with their start and end apart: 2 -> 0, of which waited for: 1 -> 0; matrix products, arithmetic and copies ran while one was open for 0% -> 0% of each run, Pallas kernels for 0% -> 0%
where the time goes in v2:
time: 83.6 us; the launch traced here: 83.5 us
  Pallas kernels  80.4 us (96%)
  local copies, waits for them, and re-layouts  2.42 us (3%)
    pallas_call x1, Pallas kernels, on_device(): pl.pallas_call(whole_kernel, out_shape=[shape((TOK, 1024), BF16), shape((...  80.4 us
    unnamed x4, local copies, waits for them, and re-layouts  2.42 us

profile of v2, /device:TPU:1, one launch (start us, length us, event | category | flops | bytes accessed | tf_op | source)
XLA Modules:
  0.0 83.5 jit_solution(547655851760291282)
XLA Ops:
  0.6 80.4 %whole.1 = (bf16[128,1024]{1,0:T(8,128)(2,1)}, bf16[128,1024]{1,0:T(8,128)(2,1)}) custom-call(s32[1,128]{1,0:T(1,128)} %bitcast.5, bf16[512,1024]{1,0:T(8,128)(2,1)} %emb_ref.1, f32[7,1024]{1,0:T(8,128)} %short_ref.1, f32[128,1024]{1,0:T(8,128)} %med_ref.1, f32[16,1024]{1,0:T(8,128)} %res_ref.1, f32[16,1024]{1,0:T(8,128)} %rate_ref.1, f32[8,128]{1,0:T(8,128)} %bitcast.3, ...), custom_call_target="tpu_custom_call" | custom-call | tf_op jit(solution)/shard_map/whole/pallas_call | solution.py:418
  81.0 0.0 copy-start
  81.0 1.7 %copy.12 = bf16[128,1024]{1,0:T(8,128)(2,1)} copy(bf16[128,1024]{1,0:T(8,128)(2,1)} %get-tuple-element.4) | data formatting | bytes 524288
  82.8 0.0 copy-done
  82.8 0.7 copy.13
Async XLA Ops:
  81.0 1.7 %copy-start = (bf16[128,1024]{1,0:T(8,128)(2,1)S(1)}, bf16[128,1024]{1,0:T(8,128)(2,1)}, u32[]{:S(2)}) copy-start(bf16[128,1024]{1,0:T(8,128)(2,1)} %get-tuple-element.5) | copy-start | bytes 786436

commit v3 on v2

--- a/solution.py
+++ b/solution.py
@@ -56,9 +56,11 @@
 
 
 def whole_kernel(
-    tok_ref, emb_ref, short_ref, med_ref, res_ref, rate_ref, qg_ref, kg_ref, hy_ref, out_ref,
+    tok_ref, emb_in, short_in, med_in, res_in, rate_in, qg_ref, kg_ref, hy_ref, out_ref,
+    emb_ref, short_ref, med_ref, res_ref, rate_ref, fetch,
     near_s, far_s, e_s, sg_s, sw_s, mw_s, cf_s, lam_s, mg_s, yl_s, end_s,
     got1, got2, got3, pre_s, group_s, h_s, xt_s, ss_s, inv_s, xf_s, kn_s, vt_s, q_s, o_s,
+    peak_s, total_s, blend_s,
     sendt, recvt, send1, recv1, send2, recv2, send3, recv3, sendc, recvc, sendi, recvi, sendj, recvj,
     senda, sendx, sendo, recvx, sendr, recvr,
 ):
@@ -76,6 +78,17 @@
     barrier = pltpu.get_barrier_semaphore()
     for where in names:
         pl.semaphore_signal(barrier, inc=1, device_id=where, device_id_type=MESH)
+
+    fetches = [
+        pltpu.make_async_copy(source, target, fetch.at[n])
+        for n, (source, target) in enumerate(
+            [(rate_in, rate_ref), (res_in, res_ref), (short_in, short_ref), (med_in, med_ref), (emb_in, emb_ref)]
+        )
+    ]
+    for copy in fetches:
+        copy.start()
+    for copy in fetches:
+        copy.wait()
 
     for c in range(BLOCKS):
         lanes = slice(c * 128, (c + 1) * 128)
@@ -111,13 +124,8 @@
         return 0
 
     lax.fori_loop(9, 16, short_block, 0)
-    for copy in tokens:
-        copy.wait()
-    embed(jnp.where(seq >= 1, near_s[...], -1), emb_ref, e_s, 16, 128)
-    embed(jnp.where(seq >= 2, far_s[...], -1), emb_ref, e_s, 0, 16)
-    lax.fori_loop(0, 9, short_block, 0)
-
-    def medium_block(block, _):
+
+    def taps_of(block):
         def taps(chunk, total):
             base = 128 + 16 * block - 16 * chunk - 15
             window = sg_s[pl.ds(pl.multiple_of(8 * base, 8), 31 * 8), :].reshape(31, 8, 128)
@@ -126,7 +134,24 @@
                 total = total + weight[j][None] * window[15 - j : 31 - j]
             return total
 
-        total = lax.fori_loop(0, 8, taps, jnp.zeros((16, 8, 128), F32))
+        return taps
+
+    def medium_start(block, _):
+        total = lax.fori_loop(0, block - 1, taps_of(block), jnp.zeros((16, 8, 128), F32))
+        mg_s[rows_of(16 * block), :] = total.reshape(128, 128)
+        return 0
+
+    mg_s[0:256, :] = jnp.zeros((256, 128), F32)
+    lax.fori_loop(2, 8, medium_start, 0)
+    for copy in tokens:
+        copy.wait()
+    embed(jnp.where(seq >= 1, near_s[...], -1), emb_ref, e_s, 16, 128)
+    embed(jnp.where(seq >= 2, far_s[...], -1), emb_ref, e_s, 0, 16)
+    lax.fori_loop(0, 9, short_block, 0)
+
+    def medium_block(block, _):
+        total = mg_s[rows_of(16 * block), :].reshape(16, 8, 128)
+        total = lax.fori_loop(jnp.maximum(block - 1, 0), 8, taps_of(block), total)
         own = sg_s[rows_of(128 + 16 * block), :].reshape(16, 8, 128)
         gated = (own * total).astype(BF16).astype(F32)
         mg_s[rows_of(16 * block), :] = gated.reshape(128, 128)
@@ -236,7 +261,6 @@
 
     sources = [2 * lax.rem(y + 4 - dy, 4) + lax.rem(half + dz, 2) for dy, dz in OFFSETS]
     places = [8 * k for k in sources]
-    right, left = 8 * g + 2 * lax.rem(x + 1, 4) + core, 8 * g + 2 * lax.rem(x + 3, 4) + core
     other = 8 * g + 2 * x + 1 - core
 
     def along(b, n, semaphores, to):
@@ -248,26 +272,15 @@
         b = places[d] + i
         if d:
             landed(xf_s.at[b], recvx.at[b])
-        along(b, 3 * d, sendx, right)
-        along(b, 3 * d + 1, sendx, left)
+        for s in range(1, 4):
+            along(b, 3 * d + s - 1, sendx, 8 * g + 2 * lax.rem(x + s, 4) + core)
         along(b, 4 * d, sendo, other)
 
-    def neighbours(d):
-        b = places[d] + 2 * lax.rem(x + 3, 4) + core
-        landed(xf_s.at[b], recvx.at[b])
-        if d % 2 == 0:
-            along(b, 3 * d + 2, sendx, right)
-        along(b, 4 * d + 1, sendo, other)
-        b = places[d] + 2 * lax.rem(x + 1, 4) + core
-        landed(xf_s.at[b], recvx.at[b])
-        if d % 2 == 1:
-            along(b, 3 * d + 2, sendx, left)
-        along(b, 4 * d + 2, sendo, other)
-
-    def opposite(d):
-        b = places[d] + 2 * lax.rem(x + 2, 4) + core
-        landed(xf_s.at[b], recvx.at[b])
-        along(b, 4 * d + 3, sendo, other)
+    def from_x(d):
+        for s in (1, 3, 2):
+            b = places[d] + 2 * lax.rem(x + s, 4) + core
+            landed(xf_s.at[b], recvx.at[b])
+            along(b, 4 * d + s, sendo, other)
 
     def row_at(i_, g_):
         return 8 * i_ + 4 * lax.rem(g_, 2) + g_ // 2
@@ -314,51 +327,29 @@
         copy = remote(mine, mine, sendi.at[d], recvi.at[d], seq=8 * group_at(*OFFSETS[d]) + i)
         copy.start()
         sent.append(copy)
-    own_column(1)
-    own_column(2)
-    neighbours(0)
-    own_column(3)
-    neighbours(1)
-    opposite(0)
+    for d in range(1, 4):
+        own_column(d)
     scales_out(0)
-    neighbours(2)
-    opposite(1)
-    neighbours(3)
-    own_column(4)
-    opposite(2)
-    own_column(5)
-    neighbours(4)
-    opposite(3)
-    own_column(6)
-    neighbours(5)
-    own_column(7)
+    for d in range(4, 8):
+        own_column(d)
     scales_out(1)
-    opposite(4)
-    neighbours(6)
+    for d in range(4):
+        from_x(d)
     scales_in(0)
-    prepare(0)
-    opposite(5)
-    neighbours(7)
-    prepare(1)
-    opposite(6)
-    prepare(2)
-    opposite(7)
-    prepare(3)
+    for d in range(4):
+        prepare(d)
     for n in range(8):
         q_s[:, 128 * n : 128 * n + 128] = (normed(8 * n + i, i, n) * query_gain).astype(BF16)
-    scales_in(1)
-    for d in range(4, 8):
-        prepare(d)
 
     factor = HEAD ** (-0.5) * math.log2(math.e)
-    column = lax.broadcasted_iota(jnp.int32, (1024, 128), 1) + 128 * i
-    allowed = lax.broadcasted_iota(jnp.int32, (1024, 128), 0) <= column
-
-    def attend(n, segment, carry, diagonal):
+    ahead = lax.broadcasted_iota(jnp.int32, (1024, 128), 0) - lax.broadcasted_iota(jnp.int32, (1024, 128), 1)
+
+    def attend(n, segment, carry, masked):
         peak, total, blend = carry
-        score = jnp.dot(kn_s[segment], q_s[:, 128 * n : 128 * n + 128], preferred_element_type=F32) * factor
-        if diagonal:
-            score = jnp.where(allowed, score, -1e30)
+        query = q_s[:, pl.ds(pl.multiple_of(128 * n, 128), 128)]
+        score = jnp.dot(kn_s[segment], query, preferred_element_type=F32) * factor
+        if masked:
+            score = jnp.where(ahead <= 128 * i + 1024 * (n - segment), score, -1e30)
         new_peak = jnp.maximum(peak, jnp.max(score, axis=0, keepdims=True))
         weight = jnp.exp2(score - new_peak)
         shrink = jnp.exp2(peak - new_peak)
@@ -366,36 +357,66 @@
         blend = blend * shrink + jnp.dot(vt_s[segment], weight.astype(BF16), preferred_element_type=F32)
         return new_peak, total, blend
 
-    columns = pl.ds(pl.multiple_of(128 * g, 128), 128)
-    given = [
-        remote(o_s.at[n], out_ref.at[:, columns], sendr.at[n], recvr.at[g], seq=8 * n + i) for n in range(8)
-    ]
-    for base in (4, 0):
+    def sweep(queries, segments, carries):
+        for j in range(4):
+            for m in range(3, j - 1, -1):
+                carries[m] = attend(2 * m + queries, 2 * j + segments, carries[m], m == j)
+        return carries
+
+    for far in (1, 0):
         carries = [
             (jnp.full((1, 128), -1e30, F32), jnp.zeros((1, 128), F32), jnp.zeros((128, 128), F32))
             for _ in range(4)
         ]
-        for segment in range(base, base + 4):
-            for n in range(segment, base + 4):
-                carries[n - base] = attend(n, segment, carries[n - base], n == segment)
-        if base:
-            carries = lax.fori_loop(
-                0, base, lambda s, held: [attend(base + n, s, held[n], False) for n in range(4)], carries
-            )
-        for n in range(4):
-            o_s[base + n] = (carries[n][2] / carries[n][1]).T.astype(BF16)
-        for n in range(base, base + 4):
-            pl.when(g != n)(given[n].start)
-    out_ref[:, columns] = o_s[g]
+        carries = sweep(lax.rem(half + far, 2), half, carries)
+        for m in range(4):
+            peak_s[4 * far + m], total_s[4 * far + m], blend_s[4 * far + m] = carries[m]
+        from_x(4 + 2 * (1 - far))
+        from_x(5 + 2 * (1 - far))
+    scales_in(1)
+    for d in range(4, 8):
+        prepare(d)
+
+    columns = pl.ds(pl.multiple_of(128 * g, 128), 128)
+
+    def given(m, far):
+        n = 2 * m + lax.rem(half + far, 2)
+        place = 4 * far + m
+        return remote(o_s.at[place], out_ref.at[:, columns], sendr.at[place], recvr.at[g], seq=8 * n + i)
+
+    for far in (1, 0):
+        carries = [(peak_s[4 * far + m], total_s[4 * far + m], blend_s[4 * far + m]) for m in range(4)]
+        carries = sweep(lax.rem(half + far, 2), 1 - half, carries)
+        for m in range(4):
+            o_s[4 * far + m] = (carries[m][2] / carries[m][1]).T.astype(BF16)
+        for m in range(4):
+            if far:
+                given(m, far).start()
+            else:
+                pl.when(y != m)(given(m, far).start)
+    out_ref[:, columns] = o_s[y]
     for n in range(8):
 
         @pl.when(g != n)
         def _(n=n):
             landed(out_ref.at[:, pl.ds(128 * n, 128)], recvr.at[n])
-            given[n].wait_send()
-
+
+    for m in range(4):
+        given(m, 1).wait_send()
+        pl.when(y != m)(given(m, 0).wait_send)
     for copy in sent:
         copy.wait_send()
+
+
+def finish_kernel(hy_in, out_in, hy_ref, out_ref, semaphores):
+    copies = [
+        pltpu.make_async_copy(hy_in, hy_ref, semaphores.at[0]),
+        pltpu.make_async_copy(out_in, out_ref, semaphores.at[1]),
+    ]
+    for copy in copies:
+        copy.start()
+    for copy in copies:
+        copy.wait()
 
 
 def vmem(*shape, dtype=F32):
@@ -415,12 +436,13 @@
 ):
     shape = jax.ShapeDtypeStruct
     counts = (2, 2, 8, 8, 8, 8, 8, 8, 4, 4, 8, 8, 16, 16, 8, 24, 32, 64, 8, 8)
-    return pl.pallas_call(
+    results = pl.pallas_call(
         whole_kernel,
         out_shape=[shape((TOK, 1024), BF16), shape((TOK, 1024), BF16)],
-        in_specs=in_vmem(8),
+        in_specs=in_vmem(1) + [pl.BlockSpec(memory_space=pl.ANY)] * 5 + in_vmem(2),
         out_specs=in_vmem(2),
         scratch_shapes=[
+            vmem(512, 1024, dtype=BF16), vmem(7, 1024), vmem(128, 1024), vmem(16, 1024), vmem(16, 1024), dmas(5),
             vmem(1, 128, dtype=jnp.int32), vmem(1, 128, dtype=jnp.int32),
             vmem(2176, 128), vmem(2048, 128), vmem(64, 128), vmem(1024, 128), vmem(128, 128), vmem(128, 128),
             vmem(1024, 128), vmem(1024, 128), vmem(128, 128),
@@ -428,6 +450,7 @@
             vmem(1024, 128), vmem(8, 128, 128, dtype=BF16), vmem(4, 1, 128), vmem(64, 1, 128),
             vmem(64, 128, 128, dtype=BF16), vmem(8, 1024, 128, dtype=BF16), vmem(8, 128, 1024, dtype=BF16),
             vmem(128, 1024, dtype=BF16), vmem(8, 128, 128, dtype=BF16),
+            vmem(8, 1, 128), vmem(8, 1, 128), vmem(8, 128, 128),
         ]
         + [dmas(count) for count in counts],
         compiler_params=pltpu.CompilerParams(vmem_limit_bytes=LIMIT, collective_id=0, has_side_effects=True),
@@ -436,6 +459,14 @@
         token_ids.reshape(1, TOK), embedding, short_filter, medium_filter, long_residue, long_rate,
         query_gain.reshape(8, 128), key_gain.reshape(8, 128),
     )
+    return pl.pallas_call(
+        finish_kernel,
+        out_shape=[shape((TOK, 1024), BF16), shape((TOK, 1024), BF16)],
+        in_specs=[pl.BlockSpec(memory_space=pl.ANY)] * 2,
+        out_specs=in_vmem(2),
+        scratch_shapes=[dmas(2)],
+        name="finish",
+    )(*results)
 
 
 def solution(mesh):

time: 83.6 us -> 73.7 us (0.88)
  the two profiles are of different devices: /device:TPU:1 before, /device:TPU:25 now
where the time goes in v3:
time: 73.7 us; the launch traced here: 73.5 us
  Pallas kernels  72.9 us (99%)
    pallas_call x1, Pallas kernels, on_device(): pl.pallas_call(whole_kernel, out_shape=[shape((TOK, 1024), BF16), shape((...  71 us
    pallas_call x1, Pallas kernels, on_device(): pl.pallas_call(finish_kernel, out_shape=[shape((TOK, 1024), BF16), shape(...  1.84 us

profile of v3, /device:TPU:25, one launch (start us, length us, event | category | flops | bytes accessed | tf_op | source)
XLA Modules:
  0.0 73.5 jit_solution(15641916467426924048)
XLA Ops:
  0.6 71.0 %whole.1 = (bf16[128,1024]{1,0:T(8,128)(2,1)}, bf16[128,1024]{1,0:T(8,128)(2,1)}) custom-call(s32[1,128]{1,0:T(1,128)} %bitcast.5, bf16[512,1024]{1,0:T(8,128)(2,1)} %emb_in.1, f32[7,1024]{1,0:T(8,128)} %short_in.1, f32[128,1024]{1,0:T(8,128)} %med_in.1, f32[16,1024]{1,0:T(8,128)} %res_in.1, f32[16,1024]{1,0:T(8,128)} %rate_in.1, f32[8,128]{1,0:T(8,128)} %bitcast.3, ...), custom_call_target="tpu_custom_call" | custom-call | tf_op jit(solution)/shard_map/whole/pallas_call | solution.py:439
  71.7 1.8 %finish.1 = (bf16[128,1024]{1,0:T(8,128)(2,1)}, bf16[128,1024]{1,0:T(8,128)(2,1)}) custom-call(bf16[128,1024]{1,0:T(8,128)(2,1)} %get-tuple-element.4.hy_in, bf16[128,1024]{1,0:T(8,128)(2,1)} %get-tuple-element.5.out_in), custom_call_target="tpu_custom_call" | custom-call | tf_op jit(solution)/shard_map/finish/pallas_call | solution.py:462

commit v4 on v3

--- a/solution.py
+++ b/solution.py
@@ -62,7 +62,7 @@
     got1, got2, got3, pre_s, group_s, h_s, xt_s, ss_s, inv_s, xf_s, kn_s, vt_s, q_s, o_s,
     peak_s, total_s, blend_s,
     sendt, recvt, send1, recv1, send2, recv2, send3, recv3, sendc, recvc, sendi, recvi, sendj, recvj,
-    senda, sendx, sendo, recvx, sendr, recvr,
+    senda, sendx, recva, recvb, recvo, sendr, recvr,
 ):
     seq, g, i = here()
     ch = lax.axis_index("ch")
@@ -86,6 +86,13 @@
         )
     ]
     for copy in fetches:
+        copy.start()
+    pl.semaphore_wait(barrier, len(names))
+    tokens = [
+        remote(tok_ref, near_s, sendt.at[0], recvt.at[0], seq=lax.rem(seq + 1, 64)),
+        remote(tok_ref, far_s, sendt.at[1], recvt.at[1], seq=lax.rem(seq + 2, 64)),
+    ]
+    for copy in tokens:
         copy.start()
     for copy in fetches:
         copy.wait()
@@ -105,14 +112,6 @@
     lam_s[...] = jnp.exp(-rate)
     embed(tok_ref[...], emb_ref, e_s, 144, 128)
 
-    pl.semaphore_wait(barrier, len(names))
-    tokens = [
-        remote(tok_ref, near_s, sendt.at[0], recvt.at[0], seq=lax.rem(seq + 1, 64)),
-        remote(tok_ref, far_s, sendt.at[1], recvt.at[1], seq=lax.rem(seq + 2, 64)),
-    ]
-    for copy in tokens:
-        copy.start()
-
     def short_block(block, _):
         first = 16 + block * 16
         own = e_s[rows_of(first), :].reshape(16, 8, 128)
@@ -174,12 +173,11 @@
     for r in range(16):
         end_s[pl.ds(r, 8, stride=16), :] = state[r]
 
-    first_scan, second_scan, third_scan = [], [], []
+    seven = pl.ds(0, 112)
     for d in range(1, 8):
         k = lax.rem(i + d, 8)
-        copy = remote(end_s.at[part(k), :], got1.at[part(i), :], send1.at[d], recv1.at[d], seq=8 * g + k)
-        copy.start()
-        first_scan.append(copy)
+        copy = remote(end_s.at[part(k), :], got1.at[part(i), :], send1.at[0], recv1.at[0], seq=8 * g + k)
+        copy.start()
     got1[part(i), :] = end_s[part(i), :]
 
     def local(block, state):
@@ -193,8 +191,8 @@
     rate = rate_ref[:, pl.ds(pl.multiple_of(128 * i, 128), 128)]
     block_decay = jnp.exp(-128.0 * rate)
     group_decay = jnp.exp(-1024.0 * rate)
-    for copy in first_scan:
-        copy.wait()
+    landed(got1.at[seven, :], send1.at[0])
+    landed(got1.at[seven, :], recv1.at[0])
     running = jnp.zeros((16, 128), F32)
     for k in range(8):
         pre_s[16 * k : 16 * k + 16, :] = running
@@ -202,12 +200,11 @@
     group_s[...] = running
     for d in range(7, 0, -1):
         k = group_at(*OFFSETS[d])
-        copy = remote(group_s, got2.at[part(g), :], send2.at[d], recv2.at[d], seq=8 * k + i)
-        copy.start()
-        second_scan.append(copy)
+        copy = remote(group_s, got2.at[part(g), :], send2.at[0], recv2.at[0], seq=8 * k + i)
+        copy.start()
     got2[part(g), :] = running
-    for copy in second_scan:
-        copy.wait()
+    landed(got2.at[seven, :], send2.at[0])
+    landed(got2.at[seven, :], recv2.at[0])
     before = jnp.zeros((16, 128), F32)
     for k in range(8):
         before = jnp.where(k < g, group_decay * before + got2[16 * k : 16 * k + 16, :], before)
@@ -216,12 +213,11 @@
         before = before * block_decay
     for d in range(1, 8):
         k = lax.rem(i + d, 8)
-        copy = remote(pre_s.at[part(k), :], got3.at[part(i), :], send3.at[d], recv3.at[d], seq=8 * g + k)
-        copy.start()
-        third_scan.append(copy)
+        copy = remote(pre_s.at[part(k), :], got3.at[part(i), :], send3.at[0], recv3.at[0], seq=8 * g + k)
+        copy.start()
     got3[part(i), :] = pre_s[part(i), :]
-    for copy in third_scan:
-        copy.wait()
+    landed(got3.at[seven, :], send3.at[0])
+    landed(got3.at[seven, :], recv3.at[0])
 
     state = jnp.stack([got3[pl.ds(r, 8, stride=16), :] for r in range(16)], axis=0)
 
@@ -244,62 +240,50 @@
         hy_ref[:, c * 128 : (c + 1) * 128] = block.astype(BF16)
     ss_s[ch] = jnp.sum(squares, axis=0, keepdims=True)
 
-    sums = []
     for d in range(1, 4):
         k = lax.rem(ch + d, 4)
-        copy = remote(ss_s.at[ch], ss_s.at[ch], sendc.at[d], recvc.at[d], ch=k)
-        copy.start()
-        sums.append(copy)
+        copy = remote(ss_s.at[ch], ss_s.at[ch], sendc.at[0], recvc.at[0], ch=k)
+        copy.start()
     slot = 8 * g + i
-    sent = []
     for d in range(7, 0, -1):
         k = group_at(*OFFSETS[d])
-        copy = remote(xt_s.at[k], xf_s.at[slot], senda.at[d], recvx.at[slot], seq=8 * k + i)
-        copy.start()
-        sent.append(copy)
+        copy = remote(xt_s.at[k], xf_s.at[slot], senda.at[0], recva.at[d], seq=8 * k + i)
+        copy.start()
     xf_s[slot] = xt_s[g]
 
     sources = [2 * lax.rem(y + 4 - dy, 4) + lax.rem(half + dz, 2) for dy, dz in OFFSETS]
     places = [8 * k for k in sources]
     other = 8 * g + 2 * x + 1 - core
 
-    def along(b, n, semaphores, to):
-        copy = remote(xf_s.at[b], xf_s.at[b], semaphores.at[n], recvx.at[b], seq=to)
-        copy.start()
-        sent.append(copy)
+    def along(b, to, receive):
+        remote(xf_s.at[b], xf_s.at[b], sendx.at[0], receive, seq=to).start()
 
     def own_column(d):
         b = places[d] + i
         if d:
-            landed(xf_s.at[b], recvx.at[b])
+            landed(xf_s.at[b], recva.at[d])
         for s in range(1, 4):
-            along(b, 3 * d + s - 1, sendx, 8 * g + 2 * lax.rem(x + s, 4) + core)
-        along(b, 4 * d, sendo, other)
+            along(b, 8 * g + 2 * lax.rem(x + s, 4) + core, recvb.at[d])
+        along(b, other, recvo.at[d])
 
     def from_x(d):
+        landed(xf_s.at[pl.ds(0, 3)], recvb.at[d])
         for s in (1, 3, 2):
-            b = places[d] + 2 * lax.rem(x + s, 4) + core
-            landed(xf_s.at[b], recvx.at[b])
-            along(b, 4 * d + s, sendo, other)
+            along(places[d] + 2 * lax.rem(x + s, 4) + core, other, recvo.at[d])
 
     def row_at(i_, g_):
         return 8 * i_ + 4 * lax.rem(g_, 2) + g_ // 2
 
     def scales_out(z):
         rows = pl.ds(8 * i + 4 * lax.rem(half + z, 2), 4)
-        for d in range(4 * z, 4 * z + 4):
-            if d:
-                landed(inv_s.at[row_at(i, sources[d])], recvi.at[d])
+        landed(inv_s.at[pl.ds(0, 3 + z)], recvi.at[z])
         for d in range(1, 8):
             to = 8 * g + lax.rem(i + d, 8)
-            copy = remote(inv_s.at[rows], inv_s.at[rows], sendj.at[8 * z + d], recvj.at[8 * z + d], seq=to)
+            copy = remote(inv_s.at[rows], inv_s.at[rows], sendj.at[0], recvj.at[z], seq=to)
             copy.start()
-            sent.append(copy)
 
     def scales_in(z):
-        for d in range(1, 8):
-            rows = pl.ds(8 * lax.rem(i + 8 - d, 8) + 4 * lax.rem(half + z, 2), 4)
-            landed(inv_s.at[rows], recvj.at[8 * z + d])
+        landed(inv_s.at[pl.ds(0, 28)], recvj.at[z])
 
     query_gain = jnp.broadcast_to(qg_ref[pl.ds(g, 1), :], (128, 128)).T
     key_gain = jnp.broadcast_to(kg_ref[pl.ds(g, 1), :], (128, 128)).T
@@ -309,24 +293,21 @@
 
     def prepare(d):
         k = sources[d]
-        for s in range(4):
-            b = places[d] + 2 * lax.rem(x + s, 4) + 1 - core
-            landed(xf_s.at[b], recvx.at[b])
+        landed(xf_s.at[pl.ds(0, 4)], recvo.at[d])
         for n in range(8):
             rows = normed(places[d] + n, n, k)
             vt_s[k, :, 128 * n : 128 * n + 128] = rows.astype(BF16)
             kn_s[k, 128 * n : 128 * n + 128, :] = (rows * key_gain).T.astype(BF16)
 
     own_column(0)
-    for copy in sums:
-        copy.wait()
+    landed(ss_s.at[pl.ds(0, 3)], sendc.at[0])
+    landed(ss_s.at[pl.ds(0, 3)], recvc.at[0])
     total = ss_s[0] + ss_s[1] + ss_s[2] + ss_s[3]
     inv_s[row_at(i, g)] = lax.rsqrt(total / C + EPS)
     mine = inv_s.at[row_at(i, g)]
     for d in range(7, 0, -1):
-        copy = remote(mine, mine, sendi.at[d], recvi.at[d], seq=8 * group_at(*OFFSETS[d]) + i)
-        copy.start()
-        sent.append(copy)
+        copy = remote(mine, mine, sendi.at[0], recvi.at[d // 4], seq=8 * group_at(*OFFSETS[d]) + i)
+        copy.start()
     for d in range(1, 4):
         own_column(d)
     scales_out(0)
@@ -357,9 +338,11 @@
         blend = blend * shrink + jnp.dot(vt_s[segment], weight.astype(BF16), preferred_element_type=F32)
         return new_peak, total, blend
 
-    def sweep(queries, segments, carries):
+    def sweep(queries, segments, carries, chains=(3, 2, 1, 0)):
         for j in range(4):
-            for m in range(3, j - 1, -1):
+            for m in chains:
+                if m < j:
+                    continue
                 carries[m] = attend(2 * m + queries, 2 * j + segments, carries[m], m == j)
         return carries
 
@@ -382,30 +365,25 @@
     def given(m, far):
         n = 2 * m + lax.rem(half + far, 2)
         place = 4 * far + m
-        return remote(o_s.at[place], out_ref.at[:, columns], sendr.at[place], recvr.at[g], seq=8 * n + i)
-
-    for far in (1, 0):
-        carries = [(peak_s[4 * far + m], total_s[4 * far + m], blend_s[4 * far + m]) for m in range(4)]
-        carries = sweep(lax.rem(half + far, 2), 1 - half, carries)
-        for m in range(4):
+        return remote(o_s.at[place], out_ref.at[:, columns], sendr.at[0], recvr.at[0], seq=8 * n + i)
+
+    for far, chains in ((1, (1, 0)), (1, (3, 2)), (0, (3, 2, 1, 0))):
+        carries = {m: (peak_s[4 * far + m], total_s[4 * far + m], blend_s[4 * far + m]) for m in chains}
+        carries = sweep(lax.rem(half + far, 2), 1 - half, carries, chains)
+        for m in chains:
             o_s[4 * far + m] = (carries[m][2] / carries[m][1]).T.astype(BF16)
-        for m in range(4):
+        for m in chains:
             if far:
                 given(m, far).start()
             else:
                 pl.when(y != m)(given(m, far).start)
     out_ref[:, columns] = o_s[y]
-    for n in range(8):
-
-        @pl.when(g != n)
-        def _(n=n):
-            landed(out_ref.at[:, pl.ds(128 * n, 128)], recvr.at[n])
-
-    for m in range(4):
-        given(m, 1).wait_send()
-        pl.when(y != m)(given(m, 0).wait_send)
-    for copy in sent:
-        copy.wait_send()
+    landed(o_s.at[pl.ds(0, 7)], recvr.at[0])
+    landed(o_s.at[pl.ds(0, 7)], sendr.at[0])
+    landed(xf_s.at[pl.ds(0, 7)], senda.at[0])
+    landed(xf_s.at[pl.ds(0, 56)], sendx.at[0])
+    landed(inv_s.at[pl.ds(0, 7)], sendi.at[0])
+    landed(inv_s.at[pl.ds(0, 56)], sendj.at[0])
 
 
 def finish_kernel(hy_in, out_in, hy_ref, out_ref, semaphores):
@@ -435,7 +413,7 @@
     token_ids, embedding, short_filter, medium_filter, long_residue, long_rate, query_gain, key_gain
 ):
     shape = jax.ShapeDtypeStruct
-    counts = (2, 2, 8, 8, 8, 8, 8, 8, 4, 4, 8, 8, 16, 16, 8, 24, 32, 64, 8, 8)
+    counts = (2, 2, 1, 1, 1, 1, 1, 1, 1, 1, 1, 2, 1, 2, 1, 1, 8, 8, 8, 1, 1)
     results = pl.pallas_call(
         whole_kernel,
         out_shape=[shape((TOK, 1024), BF16), shape((TOK, 1024), BF16)],

time: 73.7 us -> 69.2 us (0.939)
  the two profiles are of different devices: /device:TPU:25 before, /device:TPU:1 now
where the time goes in v4:
time: 69.2 us; the launch traced here: 69.1 us
  Pallas kernels  68.4 us (99%)
    pallas_call x1, Pallas kernels, on_device(): pl.pallas_call(whole_kernel, out_shape=[shape((TOK, 1024), BF16), shape((...  66.6 us
    pallas_call x1, Pallas kernels, on_device(): pl.pallas_call(finish_kernel, out_shape=[shape((TOK, 1024), BF16), shape(...  1.84 us

profile of v4, /device:TPU:1, one launch (start us, length us, event | category | flops | bytes accessed | tf_op | source)
XLA Modules:
  0.0 69.1 jit_solution(2325838765010028028)
XLA Ops:
  0.6 66.6 %whole.1 = (bf16[128,1024]{1,0:T(8,128)(2,1)}, bf16[128,1024]{1,0:T(8,128)(2,1)}) custom-call(s32[1,128]{1,0:T(1,128)} %bitcast.5, bf16[512,1024]{1,0:T(8,128)(2,1)} %emb_in.1, f32[7,1024]{1,0:T(8,128)} %short_in.1, f32[128,1024]{1,0:T(8,128)} %med_in.1, f32[16,1024]{1,0:T(8,128)} %res_in.1, f32[16,1024]{1,0:T(8,128)} %rate_in.1, f32[8,128]{1,0:T(8,128)} %bitcast.3, ...), custom_call_target="tpu_custom_call" | custom-call | tf_op jit(solution)/shard_map/whole/pallas_call | solution.py:417
  67.2 1.8 %finish.1 = (bf16[128,1024]{1,0:T(8,128)(2,1)}, bf16[128,1024]{1,0:T(8,128)(2,1)}) custom-call(bf16[128,1024]{1,0:T(8,128)(2,1)} %get-tuple-element.4.hy_in, bf16[128,1024]{1,0:T(8,128)(2,1)} %get-tuple-element.5.out_in), custom_call_target="tpu_custom_call" | custom-call | tf_op jit(solution)/shard_map/finish/pallas_call | solution.py:440

commit v5 on v4

--- a/solution.py
+++ b/solution.py
@@ -56,8 +56,8 @@
 
 
 def whole_kernel(
-    tok_ref, emb_in, short_in, med_in, res_in, rate_in, qg_ref, kg_ref, hy_ref, out_ref,
-    emb_ref, short_ref, med_ref, res_ref, rate_ref, fetch,
+    tok_in, emb_in, short_in, med_in, res_in, rate_in, qg_in, kg_in, hy_ref, out_ref,
+    tok_ref, emb_ref, short_ref, med_ref, res_ref, rate_ref, qg_ref, kg_ref, fetch,
     near_s, far_s, e_s, sg_s, sw_s, mw_s, cf_s, lam_s, mg_s, yl_s, end_s,
     got1, got2, got3, pre_s, group_s, h_s, xt_s, ss_s, inv_s, xf_s, kn_s, vt_s, q_s, o_s,
     peak_s, total_s, blend_s,
@@ -82,11 +82,15 @@
     fetches = [
         pltpu.make_async_copy(source, target, fetch.at[n])
         for n, (source, target) in enumerate(
-            [(rate_in, rate_ref), (res_in, res_ref), (short_in, short_ref), (med_in, med_ref), (emb_in, emb_ref)]
+            [
+                (tok_in, tok_ref), (rate_in, rate_ref), (res_in, res_ref), (short_in, short_ref),
+                (med_in, med_ref), (emb_in, emb_ref), (qg_in, qg_ref), (kg_in, kg_ref),
+            ]
         )
     ]
     for copy in fetches:
         copy.start()
+    fetches[0].wait()
     pl.semaphore_wait(barrier, len(names))
     tokens = [
         remote(tok_ref, near_s, sendt.at[0], recvt.at[0], seq=lax.rem(seq + 1, 64)),
@@ -94,7 +98,7 @@
     ]
     for copy in tokens:
         copy.start()
-    for copy in fetches:
+    for copy in fetches[1:]:
         copy.wait()
 
     for c in range(BLOCKS):
@@ -417,10 +421,11 @@
     results = pl.pallas_call(
         whole_kernel,
         out_shape=[shape((TOK, 1024), BF16), shape((TOK, 1024), BF16)],
-        in_specs=in_vmem(1) + [pl.BlockSpec(memory_space=pl.ANY)] * 5 + in_vmem(2),
+        in_specs=[pl.BlockSpec(memory_space=pl.ANY)] * 8,
         out_specs=in_vmem(2),
         scratch_shapes=[
-            vmem(512, 1024, dtype=BF16), vmem(7, 1024), vmem(128, 1024), vmem(16, 1024), vmem(16, 1024), dmas(5),
+            vmem(1, 128, dtype=jnp.int32), vmem(512, 1024, dtype=BF16), vmem(7, 1024), vmem(128, 1024),
+            vmem(16, 1024), vmem(16, 1024), vmem(8, 128), vmem(8, 128), dmas(8),
             vmem(1, 128, dtype=jnp.int32), vmem(1, 128, dtype=jnp.int32),
             vmem(2176, 128), vmem(2048, 128), vmem(64, 128), vmem(1024, 128), vmem(128, 128), vmem(128, 128),
             vmem(1024, 128), vmem(1024, 128), vmem(128, 128),

time: 69.2 us -> 68.5 us (0.990)
  no operation moved by 1% of the time
where the time goes in v5:
time: 68.5 us; the launch traced here: 68.4 us
  Pallas kernels  67.8 us (99%)
    pallas_call x1, Pallas kernels, on_device(): pl.pallas_call(whole_kernel, out_shape=[shape((TOK, 1024), BF16), shape((...  65.9 us
    pallas_call x1, Pallas kernels, on_device(): pl.pallas_call(finish_kernel, out_shape=[shape((TOK, 1024), BF16), shape(...  1.84 us

profile of v5, /device:TPU:1, one launch (start us, length us, event | category | flops | bytes accessed | tf_op | source)
XLA Modules:
  0.0 68.4 jit_solution(1717435708701933655)
XLA Ops:
  0.6 65.9 %whole.1 = (bf16[128,1024]{1,0:T(8,128)(2,1)}, bf16[128,1024]{1,0:T(8,128)(2,1)}) custom-call(s32[1,128]{1,0:T(1,128)} %bitcast.5, bf16[512,1024]{1,0:T(8,128)(2,1)} %emb_in.1, f32[7,1024]{1,0:T(8,128)} %short_in.1, f32[128,1024]{1,0:T(8,128)} %med_in.1, f32[16,1024]{1,0:T(8,128)} %res_in.1, f32[16,1024]{1,0:T(8,128)} %rate_in.1, f32[8,128]{1,0:T(8,128)} %bitcast.3, ...), custom_call_target="tpu_custom_call" | custom-call | tf_op jit(solution)/shard_map/whole/pallas_call | solution.py:421
  66.6 1.8 %finish.1 = (bf16[128,1024]{1,0:T(8,128)(2,1)}, bf16[128,1024]{1,0:T(8,128)(2,1)}) custom-call(bf16[128,1024]{1,0:T(8,128)(2,1)} %get-tuple-element.4.hy_in, bf16[128,1024]{1,0:T(8,128)(2,1)} %get-tuple-element.5.out_in), custom_call_target="tpu_custom_call" | custom-call | tf_op jit(solution)/shard_map/finish/pallas_call | solution.py:445

commit v6 on v5

--- a/solution.py
+++ b/solution.py
@@ -371,7 +371,7 @@
         place = 4 * far + m
         return remote(o_s.at[place], out_ref.at[:, columns], sendr.at[0], recvr.at[0], seq=8 * n + i)
 
-    for far, chains in ((1, (1, 0)), (1, (3, 2)), (0, (3, 2, 1, 0))):
+    for far, chains in ((1, (1, 0)), (1, (3, 2)), (0, (1, 0)), (0, (3, 2))):
         carries = {m: (peak_s[4 * far + m], total_s[4 * far + m], blend_s[4 * far + m]) for m in chains}
         carries = sweep(lax.rem(half + far, 2), 1 - half, carries, chains)
         for m in chains:

time: 68.5 us -> 67.8 us (0.990)
  Pallas kernels: 67.8 us -> 67.1 us
    pallas_call x1, Pallas kernels: 65.9 us -> 65.2 us  [on_device(): pl.pallas_call(whole_kernel, out_shape=[shape((TOK, 1024), BF16), shape((...]
where the time goes in v6:
time: 67.8 us; the launch traced here: 67.7 us
  Pallas kernels  67.1 us (99%)
    pallas_call x1, Pallas kernels, on_device(): pl.pallas_call(whole_kernel, out_shape=[shape((TOK, 1024), BF16), shape((...  65.2 us
    pallas_call x1, Pallas kernels, on_device(): pl.pallas_call(finish_kernel, out_shape=[shape((TOK, 1024), BF16), shape(...  1.84 us

profile of v6, /device:TPU:1, one launch (start us, length us, event | category | flops | bytes accessed | tf_op | source)
XLA Modules:
  0.0 67.7 jit_solution(7131118305285309759)
XLA Ops:
  0.6 65.2 %whole.1 = (bf16[128,1024]{1,0:T(8,128)(2,1)}, bf16[128,1024]{1,0:T(8,128)(2,1)}) custom-call(s32[1,128]{1,0:T(1,128)} %bitcast.5, bf16[512,1024]{1,0:T(8,128)(2,1)} %emb_in.1, f32[7,1024]{1,0:T(8,128)} %short_in.1, f32[128,1024]{1,0:T(8,128)} %med_in.1, f32[16,1024]{1,0:T(8,128)} %res_in.1, f32[16,1024]{1,0:T(8,128)} %rate_in.1, f32[8,128]{1,0:T(8,128)} %bitcast.3, ...), custom_call_target="tpu_custom_call" | custom-call | tf_op jit(solution)/shard_map/whole/pallas_call | solution.py:421
  65.9 1.8 %finish.1 = (bf16[128,1024]{1,0:T(8,128)(2,1)}, bf16[128,1024]{1,0:T(8,128)(2,1)}) custom-call(bf16[128,1024]{1,0:T(8,128)(2,1)} %get-tuple-element.4.hy_in, bf16[128,1024]{1,0:T(8,128)(2,1)} %get-tuple-element.5.out_in), custom_call_target="tpu_custom_call" | custom-call | tf_op jit(solution)/shard_map/finish/pallas_call | solution.py:445
